TPU v7x, 256 devices: a whole 4x4x8 slice. The times are simulated.
256 devices in a mesh: azim: 64 (over x, y_hi, z), axial: 4 (over y_lo, core).
Axes of the slice: x: 4, y: 4 (y_hi: 2, y_lo: 2; y = y_hi * 2 + y_lo), z: 8, core: 2. Of those that a mesh axis runs over, the one named last changes fastest.
Arguments:
- rhs: float32 [64, 48, 4, 128], P('azim', None, 'axial'), may hold values from -6 to 6
- coupling: float32 [64, 48, 4, 128], P('azim', None, 'axial'), may hold values from 0.2 to 0.5
- fwd_coupling: bfloat16 [64, 48, 48, 4, 128], P('azim', None, None, 'axial'), may hold values from -1 to 1
- bwd_coupling: bfloat16 [64, 48, 48, 4, 128], P('azim', None, None, 'axial'), may hold values from -1 to 1
- block_inverse: bfloat16 [64, 48, 48, 4, 128], P('azim', None, None, 'axial'), may hold values from -1 to 1
Outputs:
- correction: float32 [64, 48, 4, 128], P('azim', None, 'axial')
- remaining: float32 [64, 48, 4, 128], P('azim', None, 'axial')
All inputs are finite; a program needn't handle non-finite values.
Results may differ from a plain program's by a relative error of at most 0.0003.
Values sent between devices are 32-bit elements; how exact they have to be, the bound alone decides.
A program may use at most 128 MiB of HBM per device.

v0:
```python
import jax
import jax.numpy as jnp
from jax import lax
from jax.sharding import PartitionSpec as P

highest = lax.Precision.HIGHEST


def from_behind(value, axis, steps):
    count = lax.axis_size(axis)
    initial, last = (max(0, -steps), min(count, count - steps))
    return lax.ppermute(value, axis, [(source, source + steps) for source in range(initial, last)])


def from_root(shard, axis, root):
    mine = lax.axis_index(axis) == root
    return lax.psum(jnp.where(mine, shard, jnp.zeros_like(shard)), axis)


def extended(block, sides, width):
    for axis, dim in sides:
        count = lax.axis_size(axis)
        forward = [(i, i + 1) for i in range(count - 1)]
        backward = [(target, source) for source, target in forward]
        low = lax.ppermute(
            lax.slice_in_dim(block, block.shape[dim] - width, None, axis=dim), axis, forward
        )
        high = lax.ppermute(lax.slice_in_dim(block, 0, width, axis=dim), axis, backward)
        block = jnp.concatenate([low, block, high], axis=dim)
    return block


def cell_stride(one_block, carried, const_term):
    return const_term - jnp.einsum(
        "abl,al->bl", one_block.astype(jnp.float32), carried, precision=highest
    )


def compose_cells(blocks, sequence):
    running = None
    for position in sequence:
        one_block = blocks[position].astype(jnp.float32)
        running = -jnp.swapaxes(one_block, 0, 1)
    return running


def doubling_maps(local_map, reverse):
    size = lax.axis_size("azim")
    index = lax.axis_index("azim")
    levels = []
    current = local_map
    distance = 1
    while distance < size:
        if reverse:
            moved = from_behind(current, "azim", -distance)
            exists = index + distance < size
        else:
            moved = from_behind(current, "azim", distance)
            exists = index >= distance
        levels.append((current, distance))
        current = jnp.where(
            exists, jnp.einsum("bcl,cal->bal", current, moved, precision=highest), current
        )
        distance = distance * 2
    return (levels, current)


def doubling_entries(map_levels, local_offset, reverse):
    levels, final_map = map_levels
    size = lax.axis_size("azim")
    index = lax.axis_index("azim")
    running = local_offset
    for current, distance in levels:
        if reverse:
            moved = from_behind(running, "azim", -distance)
        else:
            moved = from_behind(running, "azim", distance)
        running = jnp.einsum("bcl,cl->bl", current, moved, precision=highest) + running
    if reverse:
        wrapped = from_root(running, "azim", 0)
    else:
        wrapped = from_root(running, "azim", size - 1)
    leaving = jnp.einsum("bcl,cl->bl", final_map, wrapped, precision=highest) + running
    if reverse:
        shifted = from_behind(leaving, "azim", -1)
        first_device = index == size - 1
    else:
        shifted = from_behind(leaving, "azim", 1)
        first_device = index == 0
    return jnp.where(first_device, wrapped, shifted)


def sweep(blocks, consts, map_levels, reverse):
    cell_count = blocks.shape[0]
    sequence = list(range(cell_count))
    if reverse:
        sequence = sequence[::-1]
    carried = jnp.zeros(consts.shape[1:], jnp.float32)
    for position in sequence:
        carried = cell_stride(blocks[position], carried, consts[position])
    local_offset = carried
    incoming_maps = doubling_entries(map_levels, local_offset, reverse)
    outputs = [None] * cell_count
    carried = incoming_maps
    for position in sequence:
        carried = cell_stride(blocks[position], carried, consts[position])
        outputs[position] = carried
    return jnp.stack(outputs)


def on_device(rhs, coupling, fwd_coupling, bwd_coupling, block_inverse):
    cell_count, block_width, _, position_total, radial_count = fwd_coupling.shape
    line_count = position_total * radial_count
    forward_blocks = fwd_coupling.reshape(cell_count, block_width, block_width, line_count)
    backward_blocks = bwd_coupling.reshape(cell_count, block_width, block_width, line_count)
    inverse_blocks = block_inverse.reshape(cell_count, block_width, block_width, line_count)
    source = rhs.reshape(cell_count, block_width, line_count)
    coupling_field = coupling.reshape(cell_count, block_width, line_count)
    forward_map = compose_cells(forward_blocks, list(range(cell_count)))
    backward_map = compose_cells(backward_blocks, list(range(cell_count))[::-1])
    forward_levels = None
    backward_levels = None
    forward_levels = doubling_maps(forward_map, False)
    backward_levels = doubling_maps(backward_map, True)

    def precondition(vector):
        consts = jnp.stack(
            [
                jnp.einsum(
                    "abl,al->bl",
                    inverse_blocks[0].astype(jnp.float32),
                    vector[0],
                    precision=highest,
                )
            ]
        )
        forward = sweep(forward_blocks, consts, forward_levels, False)
        return sweep(backward_blocks, forward, backward_levels, True)

    def stations_sum(field):
        grid = field.reshape(cell_count, block_width, position_total, radial_count)
        padded = extended(grid, (("axial", 2),), 1)
        return (padded[:, :, :-2] + padded[:, :, 2:]).reshape(cell_count, block_width, line_count)

    applied_once = precondition(source)
    middle = source - applied_once + coupling_field * stations_sum(applied_once)
    second = precondition(middle)
    correction = applied_once + second
    remaining = middle - second + coupling_field * stations_sum(second)
    return (correction.reshape(rhs.shape), remaining.reshape(rhs.shape))


def solution(mesh):
    return jax.shard_map(
        on_device,
        mesh=mesh,
        in_specs=(
            P("azim", None, "axial", None),
            P("azim", None, "axial", None),
            P("azim", None, None, "axial", None),
            P("azim", None, None, "axial", None),
            P("azim", None, None, "axial", None),
        ),
        out_specs=(P("azim", None, "axial", None), P("azim", None, "axial", None)),
        check_vma=False,
    )
```

profile of v0, /device:TPU:1, one launch (start us, length us, event | category | flops | bytes accessed | tf_op | source)
XLA Modules:
  0.0 2142.2 jit_solution(16091125914390163233)
XLA Ops:
  7.7 5.4 collective-permute-start.2
  19.5 17.9 collective-permute-done
  38.6 5.6 collective-permute-start.1
  48.5 7.0 multiply_reduce_fusion.26
  57.5 8.3 collective-permute-start.4
  65.9 5.0 collective-permute-start.3
  71.0 42.8 %collective-permute-done.3 = f32[48,128]{1,0:T(8,128)S(1)} collective-permute-done((f32[48,128]{1,0:T(8,128)S(1)}, f32[48,128]{1,0:T(8,128)S(1)}, u32[]{:S(2)}, u32[]{:S(2)}) %collective-permute-start.3) | collective-permute-done | bytes 24608 | tf_op jit(solution)/shard_map/ppermute | solution.py:12
  117.1 6.5 multiply_reduce_fusion.25
  126.8 9.3 collective-permute-start.6
  136.2 6.0 collective-permute-start.5
  143.2 17.2 collective-permute-done.6
  163.7 9.3 multiply_reduce_fusion.24
  176.3 38.1 %collective-permute-start.8 = (f32[48,48,128]{2,1,0:T(8,128)}, f32[48,48,128]{2,1,0:T(8,128)}, u32[]{:S(2)}, u32[]{:S(2)}) collective-permute-start(f32[48,48,128]{2,1,0:T(8,128)} %copy.30), channel_id=1, source_target_pairs={{0,32},{4,36},{8,40},{12,44},{16,48},{20,52},{24,56},{28,60},{32,6... | collective-permute-start | bytes 3538952 | tf_op jit(solution)/shard_map/ppermute | solution.py:12
  218.1 17.8 collective-permute-done.8
  239.2 9.4 multiply_reduce_fusion.23
  251.8 9.1 collective-permute-start.10
  261.0 3.8 collective-permute-start.9
  264.9 16.8 collective-permute-done.9
  285.1 9.3 multiply_reduce_fusion.22
  297.6 6.4 collective-permute-start.11
  317.1 319.2 %psum.28 = f32[48,128]{1,0:T(8,128)S(1)} all-reduce(f32[48,128]{1,0:T(8,128)S(1)} %broadcast_select_fusion.2), channel_id=1, replica_groups=mesh['azim'=64,'axial'=4] {'azim'}, use_global_device_ids=true, to_apply=%region_0.1 | all-reduce | flops 6144 | bytes 49152 | tf_op jit(solution)/shard_map/psum | solution.py:17
  639.8 9.3 multiply_reduce_fusion.21
  668.1 8.6 multiply_reduce_fusion.19
  682.8 7.7 collective-permute-done.16
  690.6 19.6 collective-permute-done.17
  713.5 9.3 multiply_reduce_fusion.18
  728.7 5.9 collective-permute-done.18
  734.7 12.6 collective-permute-done.19
  750.6 9.5 multiply_reduce_fusion.17
  766.2 12.0 collective-permute-done.20
  778.4 3.7 collective-permute-done.21
  785.4 9.4 multiply_reduce_fusion.16
  800.7 5.2 collective-permute-done.22
  805.9 9.6 collective-permute-done.23
  818.8 9.5 multiply_reduce_fusion.15
  832.8 343.0 %psum.29 = f32[48,128]{1,0:T(8,128)S(1)} all-reduce(f32[48,128]{1,0:T(8,128)S(1)} %broadcast_select_fusion), channel_id=1, replica_groups=mesh['azim'=64,'axial'=4] {'azim'}, use_global_device_ids=true, to_apply=%region_1.2 | all-reduce | flops 6144 | bytes 49152 | tf_op jit(solution)/shard_map/psum | solution.py:17
  1179.3 9.3 multiply_reduce_fusion.14
  1195.8 108.7 %collective-permute-start.27 = (f32[1,48,1,128]{3,1,2,0:T(8,128)S(1)}, f32[1,48,1,128]{3,1,2,0:T(8,128)S(1)}, u32[]{:S(2)}, u32[]{:S(2)}) collective-permute-start(f32[1,48,1,128]{3,1,2,0:T(8,128)S(1)} %subtract_bitcast_fusion.5), channel_id=1, source_target_pairs={{1,0},{2,1},{3,2},{5,4},{6,5},{7,6},{9,8},{10,9},{11,10},{13,12},{... | collective-permute-start | bytes 73736 | tf_op jit(solution)/shard_map/ppermute | solution.py:28
  1319.0 5.7 collective-permute-start.30
  1328.2 4.9 collective-permute-start.31
  1342.4 4.0 collective-permute-start.33
  1348.5 300.0 %psum.30 = f32[48,128]{1,0:T(8,128)S(1)} all-reduce(f32[48,128]{1,0:T(8,128)S(1)} %broadcast_select_fusion.1), channel_id=1, replica_groups=mesh['azim'=64,'axial'=4] {'azim'}, use_global_device_ids=true, to_apply=%region_2.3 | all-reduce | flops 6144 | bytes 49152 | tf_op jit(solution)/shard_map/psum | solution.py:17
  1664.4 4.0 collective-permute-done.36
  1671.2 7.5 collective-permute-done.37
  1682.6 5.1 collective-permute-done.38
  1697.7 4.8 collective-permute-done.40
  1703.7 296.5 %psum.31 = f32[48,128]{1,0:T(8,128)S(1)} all-reduce(f32[48,128]{1,0:T(8,128)S(1)} %broadcast_select_fusion.3), channel_id=1, replica_groups=mesh['azim'=64,'axial'=4] {'azim'}, use_global_device_ids=true, to_apply=%region_3.4 | all-reduce | flops 6144 | bytes 49152 | tf_op jit(solution)/shard_map/psum | solution.py:17
  2008.5 128.7 %collective-permute-start.43 = (f32[1,48,1,128]{3,1,2,0:T(8,128)S(1)}, f32[1,48,1,128]{3,1,2,0:T(8,128)S(1)}, u32[]{:S(2)}, u32[]{:S(2)}) collective-permute-start(f32[1,48,1,128]{3,1,2,0:T(8,128)S(1)} %subtract_bitcast_fusion.4), channel_id=1, source_target_pairs={{1,0},{2,1},{3,2},{5,4},{6,5},{7,6},{9,8},{10,9},{11,10},{13,12},{... | collective-permute-start | bytes 73736 | tf_op jit(solution)/shard_map/ppermute | solution.py:28
  (236 shorter events, 215.7 us)
Async XLA Ops:
  2.5 35.1 %copy-start.5 = (bf16[1,48,48,1,128]{2,1,4,3,0:T(8,128)(2,1)}, bf16[1,48,48,1,128]{2,1,4,3,0:T(8,128)(2,1)S(1)}, u32[]{:S(2)}) copy-start(bf16[1,48,48,1,128]{2,1,4,3,0:T(8,128)(2,1)S(1)} %copy.21) | copy-start | bytes 1769476
  7.7 37.5 %collective-permute-start.2 = (f32[48,48,128]{2,1,0:T(8,128)}, f32[48,48,128]{2,1,0:T(8,128)}, u32[]{:S(2)}, u32[]{:S(2)}) collective-permute-start(f32[48,48,128]{2,1,0:T(8,128)} %copy.22), channel_id=1, source_target_pairs={{0,4},{4,8},{8,12},{12,16},{16,20},{20,24},{24,28},{28,32},{32,36}... | collective-permute-start | bytes 3538952 | tf_op jit(solution)/shard_map/ppermute | solution.py:12
  15.0 30.3 %copy-start.6 = (bf16[128,48,48]{2,1,0:T(8,128)(2,1)}, bf16[128,48,48]{2,1,0:T(8,128)(2,1)S(1)}, u32[]{:S(2)}) copy-start(bf16[128,48,48]{2,1,0:T(8,128)(2,1)S(1)} %copy.68) | copy-start | bytes 1769476
  17.0 20.5 collective-permute-start
  38.6 6.5 collective-permute-start.1
  57.5 56.3 %collective-permute-start.4 = (f32[48,48,128]{2,1,0:T(8,128)}, f32[48,48,128]{2,1,0:T(8,128)}, u32[]{:S(2)}, u32[]{:S(2)}) collective-permute-start(f32[48,48,128]{2,1,0:T(8,128)} %copy.24), channel_id=1, source_target_pairs={{0,8},{4,12},{8,16},{12,20},{16,24},{20,28},{24,32},{28,36},{32,40... | collective-permute-start | bytes 3538952 | tf_op jit(solution)/shard_map/ppermute | solution.py:12
  65.9 47.8 %collective-permute-start.3 = (f32[48,128]{1,0:T(8,128)S(1)}, f32[48,128]{1,0:T(8,128)S(1)}, u32[]{:S(2)}, u32[]{:S(2)}) collective-permute-start(f32[48,128]{1,0:T(8,128)S(1)} %bitcast_add_fusion.29), channel_id=1, source_target_pairs={{0,16},{4,20},{8,24},{12,28},{16,32},{20,36},{24,40},{28,44},{32,4... | collective-permute-start | bytes 73736 | tf_op jit(solution)/shard_map/ppermute | solution.py:12
  126.8 33.5 %collective-permute-start.6 = (f32[48,48,128]{2,1,0:T(8,128)}, f32[48,48,128]{2,1,0:T(8,128)}, u32[]{:S(2)}, u32[]{:S(2)}) collective-permute-start(f32[48,48,128]{2,1,0:T(8,128)} %copy.27), channel_id=1, source_target_pairs={{0,16},{4,20},{8,24},{12,28},{16,32},{20,36},{24,40},{28,44},{32,4... | collective-permute-start | bytes 3538952 | tf_op jit(solution)/shard_map/ppermute | solution.py:12
  136.2 6.9 collective-permute-start.5
  176.3 59.7 %collective-permute-start.8 = (f32[48,48,128]{2,1,0:T(8,128)}, f32[48,48,128]{2,1,0:T(8,128)}, u32[]{:S(2)}, u32[]{:S(2)}) collective-permute-start(f32[48,48,128]{2,1,0:T(8,128)} %copy.30), channel_id=1, source_target_pairs={{0,32},{4,36},{8,40},{12,44},{16,48},{20,52},{24,56},{28,60},{32,6... | collective-permute-start | bytes 3538952 | tf_op jit(solution)/shard_map/ppermute | solution.py:12
  214.5 3.5 collective-permute-start.7
  251.8 30.0 %collective-permute-start.10 = (f32[48,48,128]{2,1,0:T(8,128)}, f32[48,48,128]{2,1,0:T(8,128)}, u32[]{:S(2)}, u32[]{:S(2)}) collective-permute-start(f32[48,48,128]{2,1,0:T(8,128)} %copy.33), channel_id=1, source_target_pairs={{0,64},{4,68},{8,72},{12,76},{16,80},{20,84},{24,88},{28,92},{32,9... | collective-permute-start | bytes 3538952 | tf_op jit(solution)/shard_map/ppermute | solution.py:12
  261.0 20.6 collective-permute-start.9
  297.6 338.9 %collective-permute-start.11 = (f32[48,48,128]{2,1,0:T(8,128)}, f32[48,48,128]{2,1,0:T(8,128)}, u32[]{:S(2)}, u32[]{:S(2)}) collective-permute-start(f32[48,48,128]{2,1,0:T(8,128)} %copy.36), channel_id=1, source_target_pairs={{0,128},{4,132},{8,136},{12,140},{16,144},{20,148},{24,152},{28,15... | collective-permute-start | bytes 3538952 | tf_op jit(solution)/shard_map/ppermute | solution.py:12
  313.1 350.7 %collective-permute-start.15 = (f32[48,48,128]{2,1,0:T(8,128)}, f32[48,48,128]{2,1,0:T(8,128)}, u32[]{:S(2)}, u32[]{:S(2)}) collective-permute-start(f32[48,48,128]{2,1,0:T(8,128)} %copy.40), channel_id=1, source_target_pairs={{4,0},{8,4},{12,8},{16,12},{20,16},{24,20},{28,24},{32,28},{36,32}... | collective-permute-start | bytes 3538952 | tf_op jit(solution)/shard_map/ppermute | solution.py:12
  649.2 3.8 collective-permute-start.12
  655.3 4.9 collective-permute-start.13
  662.5 5.5 collective-permute-start.14
  680.0 30.3 %collective-permute-start.17 = (f32[48,48,128]{2,1,0:T(8,128)}, f32[48,48,128]{2,1,0:T(8,128)}, u32[]{:S(2)}, u32[]{:S(2)}) collective-permute-start(f32[48,48,128]{2,1,0:T(8,128)} %copy.42), channel_id=1, source_target_pairs={{8,0},{12,4},{16,8},{20,12},{24,16},{28,20},{32,24},{36,28},{40,32... | collective-permute-start | bytes 3538952 | tf_op jit(solution)/shard_map/ppermute | solution.py:12
  681.3 9.2 collective-permute-start.16
  726.1 21.3 collective-permute-start.19
  727.4 7.2 collective-permute-start.18
  763.3 18.8 collective-permute-start.21
  764.7 13.6 collective-permute-start.20
  798.0 17.5 collective-permute-start.23
  799.4 6.5 collective-permute-start.22
  831.5 344.5 %collective-permute-start.24 = (f32[48,48,128]{2,1,0:T(8,128)}, f32[48,48,128]{2,1,0:T(8,128)}, u32[]{:S(2)}, u32[]{:S(2)}) collective-permute-start(f32[48,48,128]{2,1,0:T(8,128)} %copy.54), channel_id=1, source_target_pairs={{128,0},{132,4},{136,8},{140,12},{144,16},{148,20},{152,24},{156,2... | collective-permute-start | bytes 3538952 | tf_op jit(solution)/shard_map/ppermute | solution.py:12
  1179.3 128.4 %copy-start.9 = (f32[1,48,1,128]{3,2,1,0:T(1,128)S(1)}, f32[1,48,1,128]{3,2,1,0:T(1,128)}, u32[]{:S(2)}) copy-start(f32[1,48,1,128]{3,2,1,0:T(1,128)} %param.6) | copy-start | bytes 73732
  1188.6 4.9 collective-permute-start.25
  1195.8 110.7 %collective-permute-start.27 = (f32[1,48,1,128]{3,1,2,0:T(8,128)S(1)}, f32[1,48,1,128]{3,1,2,0:T(8,128)S(1)}, u32[]{:S(2)}, u32[]{:S(2)}) collective-permute-start(f32[1,48,1,128]{3,1,2,0:T(8,128)S(1)} %subtract_bitcast_fusion.5), channel_id=1, source_target_pairs={{1,0},{2,1},{3,2},{5,4},{6,5},{7,6},{9,8},{10,9},{11,10},{13,12},{... | collective-permute-start | bytes 73736 | tf_op jit(solution)/shard_map/ppermute | solution.py:28
  1304.6 3.1 collective-permute-start.26
  1308.9 2.3 collective-permute-start.28
  1313.5 4.3 collective-permute-start.29
  1319.0 6.7 collective-permute-start.30
  1328.2 5.8 collective-permute-start.31
  1335.2 4.6 collective-permute-start.32
  1342.4 4.9 collective-permute-start.33
  1651.2 2.2 collective-permute-start.34
  1655.8 4.8 collective-permute-start.35
  1663.0 5.5 collective-permute-start.36
  1669.6 9.0 collective-permute-start.37
  1681.3 6.4 collective-permute-start.38
  1688.8 5.0 collective-permute-start.39
  1696.4 6.1 collective-permute-start.40
  1703.6 303.9 %copy-start.7 = (bf16[128,48,48]{2,1,0:T(8,128)(2,1)S(1)}, bf16[128,48,48]{2,1,0:T(8,128)(2,1)}, u32[]{:S(2)}) copy-start(bf16[128,48,48]{2,1,0:T(8,128)(2,1)} %copy.127) | copy-start | bytes 1769476
  2002.8 4.6 collective-permute-start.41
  2008.5 131.9 %collective-permute-start.43 = (f32[1,48,1,128]{3,1,2,0:T(8,128)S(1)}, f32[1,48,1,128]{3,1,2,0:T(8,128)S(1)}, u32[]{:S(2)}, u32[]{:S(2)}) collective-permute-start(f32[1,48,1,128]{3,1,2,0:T(8,128)S(1)} %subtract_bitcast_fusion.4), channel_id=1, source_target_pairs={{1,0},{2,1},{3,2},{5,4},{6,5},{7,6},{9,8},{10,9},{11,10},{13,12},{... | collective-permute-start | bytes 73736 | tf_op jit(solution)/shard_map/ppermute | solution.py:28
  2137.3 4.1 collective-permute-start.42
  (6 other events, 90.7 us)
where the time goes:
time: 2150 us; the launch traced here: 2140 us
  blocking collectives  1260 us (59%)
  starting transfers between devices  397 us (18%)
  waiting for transfers between devices  240 us (11%)
  matrix products  106 us (5%)
  local copies, waits for them, and re-layouts  90.9 us (4%)
  other arithmetic  47 us (2%)
    psum x4, blocking collectives, from_root(): return lax.psum(jnp.where(mine, shard, jnp.zeros_like(shard)), axis)  1260 us
    ppermute x40, waiting for transfers between devices, from_behind(): lax.ppermute(value, axis, [(source, source + steps) for source in range(i...  238 us
    ppermute x2, starting transfers between devices, extended(): lax.ppermute(lax.slice_in_dim(block, 0, width, axis=dim), axis, backward)  237 us
    ppermute x40, starting transfers between devices, from_behind(): lax.ppermute(value, axis, [(source, source + steps) for source in range(i...  155 us
    dot_general x12, matrix products, doubling_maps(): jnp.einsum('bcl,cal->bal', current, moved, precision=highest)  106 us
  transfers between devices with their start and end apart: 44, of which 35 were waited for; matrix products, arithmetic and copies ran while one was open for 2% of the time, Pallas kernels for 0%

commit v1 on v0

v1 whole, which is shorter than its diff:
```python
import functools

import jax
import jax.numpy as jnp
from jax import lax
from jax.experimental import pallas as pl
from jax.experimental.pallas import tpu as pltpu
from jax.sharding import PartitionSpec as P

MESH = pl.DeviceIdType.MESH
W = 48
L = 128
RUN = 8
PIECES = W * W // L
ROWS = PIECES * 16
CHUNKS = 2
CROWS = ROWS // CHUNKS
CPIECES = PIECES // CHUNKS
FWD, BWD, INV = 0, 1, 2


def aligned(start, size):
    return pl.ds(pl.multiple_of(start, 8), size)


def wait_bytes(ref, sem):
    pltpu.make_async_copy(ref, ref, sem).wait()


def matvec(load, vec_ref):
    def body(step, acc):
        for inner in range(8):
            a = step * 8 + inner
            block = load(a).reshape(6, 8, L)
            acc = acc + block * vec_ref[pl.ds(a, 8, stride=0), :][None]
        return acc

    acc = lax.fori_loop(0, W // 8, body, jnp.zeros((6, 8, L), jnp.float32))
    return acc.reshape(W, L)


def kernel(
    rhs, coup, fwd, bwd, inv, corr, rem,
    s1, r1, s2, r2, maps, early, inv_t,
    vec, stage, v1, w1, v2, w2, o1, p1, o2, p2, halo_out, halo_in,
    c_t, rhs_t, coup_t, first, middle,
    mz_send, mz_recv, mg_send, mg_recv, v_send, v_recv, h_send, h_recv,
):
    me = lax.axis_index("azim")
    station = lax.axis_index("axial")
    z = lax.rem(me, RUN)
    g = me // RUN
    blocks = (fwd, bwd, inv)

    def z_peer(i):
        return {"azim": g * RUN + lax.rem(z + i, RUN)}

    def g_peer(i):
        return {"azim": lax.rem(g + i, RUN) * RUN + z}

    up = {"axial": lax.rem(station + 1, 4)}
    down = {"axial": lax.rem(station + 3, 4)}

    lane = lax.broadcasted_iota(jnp.int32, (W, L), 1)
    lane_z = lax.rem(lane, RUN)
    lane_g = lane // 16

    barrier = pltpu.get_barrier_semaphore()

    def greet(i, _):
        pl.semaphore_signal(barrier, inc=1, device_id=z_peer(i), device_id_type=MESH)
        pl.semaphore_signal(barrier, inc=1, device_id=g_peer(i), device_id_type=MESH)
        return 0

    lax.fori_loop(1, RUN, greet, 0)
    pl.semaphore_signal(barrier, inc=1, device_id=up, device_id_type=MESH)
    pl.semaphore_signal(barrier, inc=1, device_id=down, device_id_type=MESH)

    def remote(src, dst, send, recv, device):
        pltpu.make_async_remote_copy(
            src_ref=src, dst_ref=dst, send_sem=send, recv_sem=recv,
            device_id=device, device_id_type=MESH,
        ).start()

    def pack(kind):
        def body(t, _):
            piece = blocks[kind][pl.ds(pl.multiple_of(t * L, L), L), :].astype(jnp.float32).T
            for zo in range(RUN):
                s1[kind, aligned(zo * ROWS + t * 16, 16)] = piece[zo * 16 : zo * 16 + 16]
            return 0

        lax.fori_loop(0, PIECES, body, 0)

    def send_z(kind):
        for chunk in range(CHUNKS):

            def body(i, _, chunk=chunk):
                to = lax.rem(z + i, RUN)
                remote(
                    s1.at[kind, aligned(to * ROWS + chunk * CROWS, CROWS)],
                    r1.at[kind, aligned(z * ROWS + chunk * CROWS, CROWS)],
                    mz_send.at[kind, chunk], mz_recv.at[kind, chunk], z_peer(i),
                )
                return 0

            lax.fori_loop(1, RUN, body, 0)
        r1[kind, aligned(z * ROWS, ROWS)] = s1[kind, aligned(z * ROWS, ROWS)]

    def forward_g(kind):
        for chunk in range(CHUNKS):
            wait_bytes(r1.at[kind, pl.ds(0, 7 * CROWS)], mz_recv.at[kind, chunk])

            def body(t, _):
                for q in range(16):
                    s2[kind, aligned((q // 2) * ROWS + t * 16 + (q % 2) * 8, 8)] = r1[
                        kind, pl.ds(t * 16 + q, 8, stride=ROWS), :
                    ]
                return 0

            lax.fori_loop(chunk * CPIECES, (chunk + 1) * CPIECES, body, 0)

            def send(i, _, chunk=chunk):
                to = lax.rem(g + i, RUN)
                remote(
                    s2.at[kind, aligned(to * ROWS + chunk * CROWS, CROWS)],
                    r2.at[kind, aligned(g * ROWS + chunk * CROWS, CROWS)],
                    mg_send.at[kind, chunk], mg_recv.at[kind, chunk], g_peer(i),
                )
                return 0

            lax.fori_loop(1, RUN, send, 0)
        r2[kind, aligned(g * ROWS, ROWS)] = s2[kind, aligned(g * ROWS, ROWS)]

    def unpack(kind):
        for chunk in range(CHUNKS):
            wait_bytes(r2.at[kind, pl.ds(0, 7 * CROWS)], mg_recv.at[kind, chunk])

            def body(t, _):
                rows = [r2[kind, aligned(run * ROWS + t * 16, 16)] for run in range(RUN)]
                piece = jnp.concatenate(rows, axis=0).T
                if kind == INV:
                    inv_t[pl.ds(pl.multiple_of(t * L, L), L), :] = piece
                else:
                    maps[kind, 0, pl.ds(pl.multiple_of(t * L, L), L), :] = -piece
                return 0

            lax.fori_loop(chunk * CPIECES, (chunk + 1) * CPIECES, body, 0)

    def earlier(value, distance, kind):
        return pltpu.roll(value, distance if kind == FWD else L - distance, 1)

    def inside(distance, kind):
        return lane_z >= distance if kind == FWD else lane_z < RUN - distance

    def compose(kind, level):
        distance = 1 << level
        exists = inside(distance, kind)
        sub = lax.broadcasted_iota(jnp.int32, (W, L), 0)

        def shift(a, _):
            moved = earlier(maps[kind, level, aligned(a * W, W)], distance, kind)
            early[aligned(a * W, W)] = jnp.where(exists, moved, jnp.where(sub == a, 1.0, 0.0))
            return 0

        lax.fori_loop(0, W, shift, 0)

        def product(four, _):
            def over(step, acc):
                acc = list(acc)
                for inner in range(8):
                    c = step * 8 + inner
                    later = maps[kind, level, aligned(c * W, W)].reshape(6, 8, L)
                    for i in range(4):
                        factor = early[pl.ds((four * 4 + i) * W + c, 8, stride=0), :]
                        acc[i] = acc[i] + later * factor[None]
                return tuple(acc)

            zero = jnp.zeros((6, 8, L), jnp.float32)
            acc = lax.fori_loop(0, W // 8, over, (zero,) * 4)
            for i in range(4):
                maps[kind, level + 1, aligned((four * 4 + i) * W, W)] = acc[i].reshape(W, L)
            return 0

        lax.fori_loop(0, W // 4, product, 0)

    def apply_map(kind, level):
        return matvec(lambda a: maps[kind, level, aligned(a * W, W)], vec)

    def sweep(kind, value):
        state = value
        for level in range(3):
            distance = 1 << level
            moved = earlier(state, distance, kind)
            vec[0:W] = jnp.where(inside(distance, kind), moved, 0.0)
            state = state + apply_map(kind, level)
        order = lane_g if kind == FWD else RUN - 1 - lane_g

        def run_step(n, carry):
            running, entering = carry
            moved = earlier(running, 16, kind)
            entering = jnp.where(order == n - RUN, moved, entering)
            vec[0:W] = moved
            return state + apply_map(kind, 3), entering

        running, entering = lax.fori_loop(1, 15, run_step, (state, jnp.zeros((W, L), jnp.float32)))
        entering = jnp.where(order == RUN - 1, earlier(running, 16, kind), entering)
        place = RUN - 1 - lane_z if kind == FWD else lane_z
        for distance in (1, 2, 4):
            back = pltpu.roll(entering, L - distance if kind == FWD else distance, 1)
            entering = jnp.where(place < distance, entering, back)
        vec[0:W] = entering
        return state + apply_map(kind, 3)

    stage[...] = jnp.zeros((2, L, L), jnp.float32)
    vec[0:W] = rhs[...]
    stage[0, 0:W] = matvec(lambda a: inv[pl.ds(pl.multiple_of(a * W, 16), W), :].astype(jnp.float32), vec)
    stage[0, W : 2 * W] = rhs[...]
    stage[1, 0:W] = coup[...]
    for block in range(2):
        turned = stage[block].T
        for zo in range(RUN):
            v1[pl.ds(zo * 32 + block * 16, 16)] = turned[zo * 16 : zo * 16 + 16]
    pack(FWD)
    pl.semaphore_wait(barrier, 16)

    def send_v1(i, _):
        to = lax.rem(z + i, RUN)
        remote(v1.at[aligned(to * 32, 32)], w1.at[aligned(z * 32, 32)], v_send.at[0], v_recv.at[0], z_peer(i))
        return 0

    lax.fori_loop(1, RUN, send_v1, 0)
    w1[aligned(z * 32, 32)] = v1[aligned(z * 32, 32)]
    send_z(FWD)
    pack(BWD)
    pack(INV)
    wait_bytes(w1.at[pl.ds(0, 7 * 32)], v_recv.at[0])
    for block in range(2):
        for q in range(16):
            v2[pl.ds((q // 2) * 32 + block * 16 + (q % 2) * 8, 8)] = w1[pl.ds(block * 16 + q, 8, stride=32), :]

    def send_v2(i, _):
        to = lax.rem(g + i, RUN)
        remote(v2.at[aligned(to * 32, 32)], w2.at[aligned(g * 32, 32)], v_send.at[1], v_recv.at[1], g_peer(i))
        return 0

    lax.fori_loop(1, RUN, send_v2, 0)
    w2[aligned(g * 32, 32)] = v2[aligned(g * 32, 32)]
    forward_g(FWD)
    send_z(BWD)
    wait_bytes(w2.at[pl.ds(0, 7 * 32)], v_recv.at[1])
    turned = [
        jnp.concatenate([w2[pl.ds(run * 32 + block * 16, 16)] for run in range(RUN)], axis=0).T for block in range(2)
    ]
    c_t[...] = turned[0][0:W]
    rhs_t[...] = turned[0][W : 2 * W]
    coup_t[...] = turned[1][0:W]

    unpack(FWD)
    compose(FWD, 0)
    compose(FWD, 1)
    forward_g(BWD)
    send_z(INV)
    compose(FWD, 2)
    halfway = sweep(FWD, c_t[...])
    c_t[...] = halfway
    unpack(BWD)
    compose(BWD, 0)
    compose(BWD, 1)
    compose(BWD, 2)
    forward_g(INV)

    def stations_sum(turn, value):
        halo_out[turn] = value
        remote(halo_out.at[turn], halo_in.at[turn, 0], h_send.at[turn, 0], h_recv.at[turn, 0], up)
        remote(halo_out.at[turn], halo_in.at[turn, 1], h_send.at[turn, 1], h_recv.at[turn, 1], down)
        for side in range(2):
            wait_bytes(halo_in.at[turn, side], h_recv.at[turn, side])
            wait_bytes(halo_out.at[turn], h_send.at[turn, side])
        below = jnp.where(station > 0, halo_in[turn, 0], 0.0)
        above = jnp.where(station < 3, halo_in[turn, 1], 0.0)
        return below + above

    first[...] = sweep(BWD, c_t[...])
    middle[...] = rhs_t[...] - first[...] + coup_t[...] * stations_sum(0, first[...])
    unpack(INV)
    vec[0:W] = middle[...]
    c_t[...] = sweep(FWD, matvec(lambda a: inv_t[aligned(a * W, W)], vec))
    second = sweep(BWD, c_t[...])
    c_t[...] = second
    stage[0, 0:W] = first[...] + second
    stage[0, W : 2 * W] = middle[...] - c_t[...] + coup_t[...] * stations_sum(1, c_t[...])

    o1[...] = stage[0].T

    def send_o1(i, _):
        to = lax.rem(g + i, RUN)
        remote(o1.at[aligned(to * 16, 16)], p1.at[aligned(g * 16, 16)], v_send.at[2], v_recv.at[2], g_peer(i))
        return 0

    lax.fori_loop(1, RUN, send_o1, 0)
    p1[aligned(g * 16, 16)] = o1[aligned(g * 16, 16)]
    wait_bytes(p1.at[pl.ds(0, 7 * 16)], v_recv.at[2])
    for q in range(16):
        o2[pl.ds(q, 8, stride=16), :] = p1[pl.ds(q * 8, 8)]

    def send_o2(i, _):
        to = lax.rem(z + i, RUN)
        remote(o2.at[aligned(to * 16, 16)], p2.at[aligned(z * 16, 16)], v_send.at[3], v_recv.at[3], z_peer(i))
        return 0

    lax.fori_loop(1, RUN, send_o2, 0)
    p2[aligned(z * 16, 16)] = o2[aligned(z * 16, 16)]
    wait_bytes(p2.at[pl.ds(0, 7 * 16)], v_recv.at[3])
    final = p2[...].T
    corr[...] = final[0:W]
    rem[...] = final[W : 2 * W]

    for kind in range(3):
        for chunk in range(CHUNKS):
            wait_bytes(s1.at[kind, pl.ds(0, 7 * CROWS)], mz_send.at[kind, chunk])
            wait_bytes(s2.at[kind, pl.ds(0, 7 * CROWS)], mg_send.at[kind, chunk])
    for at, ref in ((0, v1), (1, v2)):
        wait_bytes(ref.at[pl.ds(0, 7 * 32)], v_send.at[at])
    for at, ref in ((2, o1), (3, o2)):
        wait_bytes(ref.at[pl.ds(0, 7 * 16)], v_send.at[at])


def on_device(rhs, coupling, fwd_coupling, bwd_coupling, block_inverse):
    f32 = jnp.float32
    vmem = pl.BlockSpec(memory_space=pltpu.VMEM)
    dma = pltpu.SemaphoreType.DMA
    mat = pltpu.VMEM((3, W * W, L), f32)
    small = pltpu.VMEM((W, L), f32)
    square = pltpu.VMEM((L, L), f32)
    wide = pltpu.VMEM((2 * L, L), f32)
    corr, rem = pl.pallas_call(
        kernel,
        out_shape=(jax.ShapeDtypeStruct((W, L), f32),) * 2,
        in_specs=[vmem] * 5,
        out_specs=(vmem, vmem),
        scratch_shapes=[
            mat, pltpu.VMEM((3, W * W + ROWS, L), f32), mat, mat,
            pltpu.VMEM((2, 4, W * W, L), f32), pltpu.VMEM((W * W + 8, L), f32), pltpu.VMEM((W * W, L), f32),
            pltpu.VMEM((W + 8, L), f32), pltpu.VMEM((2, L, L), f32),
            wide, pltpu.VMEM((2 * L + 32, L), f32), wide, wide, square, square, pltpu.VMEM((L + 16, L), f32), square,
            pltpu.VMEM((2, W, L), f32), pltpu.VMEM((2, 2, W, L), f32),
            small, small, small, small, small,
            dma((3, CHUNKS)), dma((3, CHUNKS)), dma((3, CHUNKS)), dma((3, CHUNKS)),
            dma((4,)), dma((4,)), dma((2, 2)), dma((2, 2)),
        ],
        compiler_params=pltpu.CompilerParams(
            collective_id=0, has_side_effects=True, vmem_limit_bytes=48 << 20
        ),
        name="both_applies",
    )(
        rhs.reshape(W, L), coupling.reshape(W, L), fwd_coupling.reshape(W * W, L),
        bwd_coupling.reshape(W * W, L), block_inverse.reshape(W * W, L),
    )
    return corr.reshape(rhs.shape), rem.reshape(rhs.shape)


def solution(mesh):
    vector = P("azim", None, "axial", None)
    matrix = P("azim", None, None, "axial", None)
    return jax.shard_map(
        on_device,
        mesh=mesh,
        in_specs=(vector, vector, matrix, matrix, matrix),
        out_specs=(vector, vector),
        check_vma=False,
    )
```

time: 2150 us -> 150 us (0.07)
  blocking collectives: 1260 us -> 0 us
  starting transfers between devices: 397 us -> 0 us
  waiting for transfers between devices: 240 us -> 0 us
  Pallas kernels: 0 us -> 143 us
  matrix products: 106 us -> 0 us
  local copies, waits for them, and re-layouts: 90.9 us -> 5.88 us
  other arithmetic: 47 us -> 0 us
    psum x4 -> x0, blocking collectives: 1260 us -> none  [from_root(): return lax.psum(jnp.where(mine, shard, jnp.zeros_like(shard)), axis)]
    ppermute x44 -> x0, starting transfers between devices: 397 us -> none  [the longest x2 237 us: extended(): lax.ppermute(lax.slice_in_dim(block, 0, width, axis=dim), axis, backward)]
    ppermute x44 -> x0, waiting for transfers between devices: 240 us -> none  [the longest x40 238 us: from_behind(): lax.ppermute(value, axis, [(source, source + steps) for source in range(i...]
    pallas_call x0 -> x1, Pallas kernels: none -> 143 us  [on_device(): pl.pallas_call(kernel, out_shape=(jax.ShapeDtypeStruct((W, L), f32),) * 2...]
    dot_general x12 -> x0, matrix products: 106 us -> none  [doubling_maps(): jnp.einsum('bcl,cal->bal', current, moved, precision=highest)]
    ppermute x12 -> x0, local copies, waits for them, and re-layouts: 39.4 us -> none  [from_behind(): lax.ppermute(value, axis, [(source, source + steps) for source in range(i...]
    unnamed x26 -> x0, other arithmetic: 38 us -> none
    select_n x10 -> x0, local copies, waits for them, and re-layouts: 31 us -> none  [doubling_maps(): jnp.where(exists, jnp.einsum('bcl,cal->bal', current, moved, precision=hi...]
  transfers between devices with their start and end apart: 44 -> 0, of which waited for: 35 -> 0; matrix products, arithmetic and copies ran while one was open for 2% -> 0% of each run, Pallas kernels for 0% -> 0%
where the time goes in v1:
time: 150 us; the launch traced here: 149 us
  Pallas kernels  143 us (95%)
  local copies, waits for them, and re-layouts  5.88 us (4%)
    pallas_call x1, Pallas kernels, on_device(): pl.pallas_call(kernel, out_shape=(jax.ShapeDtypeStruct((W, L), f32),) * 2...  143 us
    unnamed x12, local copies, waits for them, and re-layouts  5.88 us

profile of v1, /device:TPU:1, one launch (start us, length us, event | category | flops | bytes accessed | tf_op | source)
XLA Modules:
  0.0 149.3 jit_solution(8763959342554963474)
XLA Ops:
  0.6 0.0 copy-start
  0.6 1.1 copy-done
  1.7 0.0 copy-start.1
  1.7 1.1 copy-done.1
  2.8 0.0 copy-start.2
  2.8 1.1 copy-done.2
  3.8 0.0 copy-start.3
  3.8 0.7 copy-done.3
  4.6 0.0 copy-start.4
  4.6 0.7 copy-done.4
  5.3 142.8 %both_applies.1 = (f32[48,128]{1,0:T(8,128)S(1)}, f32[48,128]{1,0:T(8,128)S(1)}) custom-call(f32[48,128]{1,0:T(8,128)S(1)} %bitcast.14, f32[48,128]{1,0:T(8,128)S(1)} %bitcast.15, bf16[2304,128]{1,0:T(8,128)(2,1)S(1)} %bitcast.11, bf16[2304,128]{1,0:T(8,128)(2,1)S(1)} %bitcast.12, bf16[2304,128]{1,0:T(8,128)(2,1)S(1)} %bitcast.13), custom_call_target="tpu_custom_call" | custom-call | tf_op jit(solution)/shard_map/both_applies/pallas_call | solution.py:336
  148.1 0.6 copy.11
  148.7 0.6 copy.12
Async XLA Ops:
  0.6 1.1 copy-start
  1.7 1.1 copy-start.1
  2.8 1.1 copy-start.2
  3.8 0.7 copy-start.3
  4.6 0.7 copy-start.4

commit v2 on v1

v2 whole, which is shorter than its diff:
```python
import functools

import jax
import jax.numpy as jnp
from jax import lax
from jax.experimental import pallas as pl
from jax.experimental.pallas import tpu as pltpu
from jax.sharding import PartitionSpec as P

MESH = pl.DeviceIdType.MESH
W = 48
L = 128
RUN = 8
PIECES = W * W // L
ROWS = PIECES * 16
CHUNKS = 3
EAGER = 2
CROWS = ROWS // CHUNKS
CPIECES = PIECES // CHUNKS
FWD, BWD, INV = 0, 1, 2


def aligned(start, size):
    return pl.ds(start if isinstance(start, int) else pl.multiple_of(start, 8), size)


def wait_bytes(ref, sem):
    pltpu.make_async_copy(ref, ref, sem).wait()


def matvec(load, vec_ref):
    acc = jnp.zeros((6, 8, L), jnp.float32)
    for a in range(W):
        acc = acc + load(a).reshape(6, 8, L) * vec_ref[pl.ds(a, 8, stride=0), :][None]
    return acc.reshape(W, L)


def kernel(
    rhs_in, coup_in, fwd_in, bwd_in, inv_in, corr, rem, rhs, coup, blocks, in_sem,
    s1, r1, s2, r2, maps, early, inv_t,
    vec, stage, v1, w1, v2, w2, o1, p1, o2, p2, halo_out, halo_in,
    c_t, rhs_t, coup_t, first, middle,
    mz_send, mz_recv, mg_send, mg_recv, v_send, v_recv, h_send, h_recv,
):
    me = lax.axis_index("azim")
    station = lax.axis_index("axial")
    z = lax.rem(me, RUN)
    g = me // RUN
    loads = [
        pltpu.make_async_copy(src, dst, in_sem.at[at])
        for at, (src, dst) in enumerate((
            (fwd_in, blocks.at[FWD]), (rhs_in, rhs), (coup_in, coup), (inv_in, blocks.at[INV]), (bwd_in, blocks.at[BWD]),
        ))
    ]
    for load in loads:
        load.start()

    def z_peer(i):
        return {"azim": g * RUN + lax.rem(z + i, RUN)}

    def g_peer(i):
        return {"azim": lax.rem(g + i, RUN) * RUN + z}

    up = {"axial": lax.rem(station + 1, 4)}
    down = {"axial": lax.rem(station + 3, 4)}

    lane = lax.broadcasted_iota(jnp.int32, (W, L), 1)
    lane_z = lax.rem(lane, RUN)
    lane_g = lane // 16

    barrier = pltpu.get_barrier_semaphore()

    def greet(i, _):
        pl.semaphore_signal(barrier, inc=1, device_id=z_peer(i), device_id_type=MESH)
        pl.semaphore_signal(barrier, inc=1, device_id=g_peer(i), device_id_type=MESH)
        return 0

    lax.fori_loop(1, RUN, greet, 0)
    pl.semaphore_signal(barrier, inc=1, device_id=up, device_id_type=MESH)
    pl.semaphore_signal(barrier, inc=1, device_id=down, device_id_type=MESH)

    def remote(src, dst, send, recv, device):
        pltpu.make_async_remote_copy(
            src_ref=src, dst_ref=dst, send_sem=send, recv_sem=recv,
            device_id=device, device_id_type=MESH,
        ).start()

    def pack(kind, chunk):
        def body(step, _):
            for inner in range(3):
                t = step * 3 + inner
                piece = blocks[kind, pl.ds(pl.multiple_of(t * L, L), L), :].astype(jnp.float32).T
                for zo in range(RUN):
                    s1[kind, aligned(zo * ROWS + t * 16, 16)] = piece[zo * 16 : zo * 16 + 16]
            return 0

        lax.fori_loop(chunk * CPIECES // 3, (chunk + 1) * CPIECES // 3, body, 0)

    def send_z(kind, chunk):
        for i in range(1, RUN):
            to = lax.rem(z + i, RUN)
            remote(
                s1.at[kind, aligned(to * ROWS + chunk * CROWS, CROWS)],
                r1.at[kind, aligned(z * ROWS + chunk * CROWS, CROWS)],
                mz_send.at[kind, chunk], mz_recv.at[kind, chunk], z_peer(i),
            )
        own = aligned(z * ROWS + chunk * CROWS, CROWS)
        r1[kind, own] = s1[kind, own]

    def forward_g(kind, chunk):
        wait_bytes(r1.at[kind, pl.ds(0, 7 * CROWS)], mz_recv.at[kind, chunk])

        def body(t, _):
            for q in range(16):
                s2[kind, aligned((q // 2) * ROWS + t * 16 + (q % 2) * 8, 8)] = r1[
                    kind, pl.ds(t * 16 + q, 8, stride=ROWS), :
                ]
            return 0

        lax.fori_loop(chunk * CPIECES, (chunk + 1) * CPIECES, body, 0)
        for i in range(1, RUN):
            to = lax.rem(g + i, RUN)
            remote(
                s2.at[kind, aligned(to * ROWS + chunk * CROWS, CROWS)],
                r2.at[kind, aligned(g * ROWS + chunk * CROWS, CROWS)],
                mg_send.at[kind, chunk], mg_recv.at[kind, chunk], g_peer(i),
            )
        own = aligned(g * ROWS + chunk * CROWS, CROWS)
        r2[kind, own] = s2[kind, own]

    def unpack(kind, chunk):
        wait_bytes(r2.at[kind, pl.ds(0, 7 * CROWS)], mg_recv.at[kind, chunk])

        def body(step, _):
            for inner in range(3):
                t = step * 3 + inner
                rows = [r2[kind, aligned(run * ROWS + t * 16, 16)] for run in range(RUN)]
                piece = jnp.concatenate(rows, axis=0).T
                if kind == INV:
                    inv_t[pl.ds(pl.multiple_of(t * L, L), L), :] = piece
                else:
                    maps[kind, 0, pl.ds(pl.multiple_of(t * L, L), L), :] = -piece
            return 0

        lax.fori_loop(chunk * CPIECES // 3, (chunk + 1) * CPIECES // 3, body, 0)

    def earlier(value, distance, kind):
        return pltpu.roll(value, distance if kind == FWD else L - distance, 1)

    def inside(distance, kind):
        return lane_z >= distance if kind == FWD else lane_z < RUN - distance

    def compose(kind, level):
        distance = 1 << level
        exists = inside(distance, kind)
        sub = lax.broadcasted_iota(jnp.int32, (W, L), 0)

        def shift(step, _):
            for inner in range(8):
                a = step * 8 + inner
                moved = earlier(maps[kind, level, aligned(a * W, W)], distance, kind)
                early[aligned(a * W, W)] = jnp.where(exists, moved, jnp.where(sub == a, 1.0, 0.0))
            return 0

        lax.fori_loop(0, W // 8, shift, 0)

        def product(four, _):
            acc = [jnp.zeros((6, 8, L), jnp.float32)] * 4
            for c in range(W):
                later = maps[kind, level, pl.ds(c * W, W)].reshape(6, 8, L)
                for i in range(4):
                    factor = early[pl.ds((four * 4 + i) * W + c, 8, stride=0), :]
                    acc[i] = acc[i] + later * factor[None]
            for i in range(4):
                maps[kind, level + 1, aligned((four * 4 + i) * W, W)] = acc[i].reshape(W, L)
            return 0

        lax.fori_loop(0, W // 4, product, 0)

    def apply_map(kind, level):
        return matvec(lambda a: maps[kind, level, pl.ds(a * W, W)], vec)

    def sweep(kind, value):
        state = value
        for level in range(3):
            distance = 1 << level
            moved = earlier(state, distance, kind)
            vec[0:W] = jnp.where(inside(distance, kind), moved, 0.0)
            state = state + apply_map(kind, level)
        order = lane_g if kind == FWD else RUN - 1 - lane_g

        def run_step(n, carry):
            running, entering = carry
            moved = earlier(running, 16, kind)
            entering = jnp.where(order == n - RUN, moved, entering)
            vec[0:W] = moved
            return state + apply_map(kind, 3), entering

        running, entering = lax.fori_loop(1, 15, run_step, (state, jnp.zeros((W, L), jnp.float32)))
        entering = jnp.where(order == RUN - 1, earlier(running, 16, kind), entering)
        place = RUN - 1 - lane_z if kind == FWD else lane_z
        for distance in (1, 2, 4):
            back = pltpu.roll(entering, L - distance if kind == FWD else distance, 1)
            entering = jnp.where(place < distance, entering, back)
        vec[0:W] = entering
        return state + apply_map(kind, 3)

    def send_vectors():
        stage[...] = jnp.zeros((2, L, L), jnp.float32)
        for load in loads[1:4]:
            load.wait()
        vec[0:W] = rhs[...]
        stage[0, 0:W] = matvec(lambda a: blocks[INV, pl.ds(a * W, W), :].astype(jnp.float32), vec)
        stage[0, W : 2 * W] = rhs[...]
        stage[1, 0:W] = coup[...]
        for block in range(2):
            turned = stage[block].T
            for zo in range(RUN):
                v1[pl.ds(zo * 32 + block * 16, 16)] = turned[zo * 16 : zo * 16 + 16]
        for i in range(1, RUN):
            to = lax.rem(z + i, RUN)
            remote(
                v1.at[aligned(to * 32, 32)], w1.at[aligned(z * 32, 32)], v_send.at[0], v_recv.at[0], z_peer(i)
            )
        w1[aligned(z * 32, 32)] = v1[aligned(z * 32, 32)]

    def forward_vectors():
        wait_bytes(w1.at[pl.ds(0, 7 * 32)], v_recv.at[0])
        for block in range(2):
            for q in range(16):
                v2[pl.ds((q // 2) * 32 + block * 16 + (q % 2) * 8, 8)] = w1[pl.ds(block * 16 + q, 8, stride=32), :]
        for i in range(1, RUN):
            to = lax.rem(g + i, RUN)
            remote(
                v2.at[aligned(to * 32, 32)], w2.at[aligned(g * 32, 32)], v_send.at[1], v_recv.at[1], g_peer(i)
            )
        w2[aligned(g * 32, 32)] = v2[aligned(g * 32, 32)]

    def take_vectors():
        wait_bytes(w2.at[pl.ds(0, 7 * 32)], v_recv.at[1])
        turned = [
            jnp.concatenate([w2[pl.ds(run * 32 + block * 16, 16)] for run in range(RUN)], axis=0).T
            for block in range(2)
        ]
        c_t[...] = turned[0][0:W]
        rhs_t[...] = turned[0][W : 2 * W]
        coup_t[...] = turned[1][0:W]

    loads[0].wait()
    for chunk in range(CHUNKS):
        pack(FWD, chunk)
        if chunk == 0:
            pl.semaphore_wait(barrier, 16)
        send_z(FWD, chunk)
    send_vectors()
    loads[4].wait()
    for chunk in range(CHUNKS):
        pack(BWD, chunk)
        if EAGER:
            send_z(BWD, chunk)
    for chunk in range(CHUNKS):
        pack(INV, chunk)
    for chunk in range(CHUNKS):
        forward_g(FWD, chunk)
    forward_vectors()
    if not EAGER:
        for chunk in range(CHUNKS):
            send_z(BWD, chunk)
    if EAGER > 1:
        for chunk in range(CHUNKS):
            send_z(INV, chunk)
    for chunk in range(CHUNKS):
        unpack(FWD, chunk)
    take_vectors()
    for level in range(3):
        compose(FWD, level)
        forward_g(BWD, level)
    c_t[...] = sweep(FWD, c_t[...])
    for chunk in range(CHUNKS):
        unpack(BWD, chunk)
    compose(BWD, 0)
    forward_g(INV, 0)
    compose(BWD, 1)
    compose(BWD, 2)
    forward_g(INV, 1)

    def stations_sum(turn, value):
        halo_out[turn] = value
        remote(halo_out.at[turn], halo_in.at[turn, 0], h_send.at[turn, 0], h_recv.at[turn, 0], up)
        remote(halo_out.at[turn], halo_in.at[turn, 1], h_send.at[turn, 1], h_recv.at[turn, 1], down)
        for side in range(2):
            wait_bytes(halo_in.at[turn, side], h_recv.at[turn, side])
            wait_bytes(halo_out.at[turn], h_send.at[turn, side])
        below = jnp.where(station > 0, halo_in[turn, 0], 0.0)
        above = jnp.where(station < 3, halo_in[turn, 1], 0.0)
        return below + above

    first[...] = sweep(BWD, c_t[...])
    middle[...] = rhs_t[...] - first[...] + coup_t[...] * stations_sum(0, first[...])
    forward_g(INV, 2)
    for chunk in range(CHUNKS):
        unpack(INV, chunk)
    vec[0:W] = middle[...]
    c_t[...] = sweep(FWD, matvec(lambda a: inv_t[pl.ds(a * W, W)], vec))
    second = sweep(BWD, c_t[...])
    c_t[...] = second
    stage[0, 0:W] = first[...] + second
    stage[0, W : 2 * W] = middle[...] - c_t[...] + coup_t[...] * stations_sum(1, c_t[...])

    o1[...] = stage[0].T

    for i in range(1, RUN):
        to = lax.rem(g + i, RUN)
        remote(o1.at[aligned(to * 16, 16)], p1.at[aligned(g * 16, 16)], v_send.at[2], v_recv.at[2], g_peer(i))
    p1[aligned(g * 16, 16)] = o1[aligned(g * 16, 16)]
    wait_bytes(p1.at[pl.ds(0, 7 * 16)], v_recv.at[2])
    for q in range(16):
        o2[pl.ds(q, 8, stride=16), :] = p1[pl.ds(q * 8, 8)]

    for i in range(1, RUN):
        to = lax.rem(z + i, RUN)
        remote(o2.at[aligned(to * 16, 16)], p2.at[aligned(z * 16, 16)], v_send.at[3], v_recv.at[3], z_peer(i))
    p2[aligned(z * 16, 16)] = o2[aligned(z * 16, 16)]
    wait_bytes(p2.at[pl.ds(0, 7 * 16)], v_recv.at[3])
    final = p2[...].T
    corr[...] = final[0:W]
    rem[...] = final[W : 2 * W]

    for kind in range(3):
        for chunk in range(CHUNKS):
            wait_bytes(s1.at[kind, pl.ds(0, 7 * CROWS)], mz_send.at[kind, chunk])
            wait_bytes(s2.at[kind, pl.ds(0, 7 * CROWS)], mg_send.at[kind, chunk])
    for at, ref in ((0, v1), (1, v2)):
        wait_bytes(ref.at[pl.ds(0, 7 * 32)], v_send.at[at])
    for at, ref in ((2, o1), (3, o2)):
        wait_bytes(ref.at[pl.ds(0, 7 * 16)], v_send.at[at])


def on_device(rhs, coupling, fwd_coupling, bwd_coupling, block_inverse):
    f32 = jnp.float32
    vmem = pl.BlockSpec(memory_space=pltpu.VMEM)
    dma = pltpu.SemaphoreType.DMA
    mat = pltpu.VMEM((3, W * W, L), f32)
    small = pltpu.VMEM((W, L), f32)
    square = pltpu.VMEM((L, L), f32)
    wide = pltpu.VMEM((2 * L, L), f32)
    corr, rem = pl.pallas_call(
        kernel,
        out_shape=(jax.ShapeDtypeStruct((W, L), f32),) * 2,
        in_specs=[pl.BlockSpec(memory_space=pl.ANY)] * 5,
        out_specs=(vmem, vmem),
        scratch_shapes=[
            small, small, pltpu.VMEM((3, W * W, L), jnp.bfloat16), dma((5,)),
            mat, pltpu.VMEM((3, W * W + ROWS, L), f32), mat, mat,
            pltpu.VMEM((2, 4, W * W, L), f32), pltpu.VMEM((W * W + 8, L), f32), pltpu.VMEM((W * W, L), f32),
            pltpu.VMEM((W + 8, L), f32), pltpu.VMEM((2, L, L), f32),
            wide, pltpu.VMEM((2 * L + 32, L), f32), wide, wide, square, square, pltpu.VMEM((L + 16, L), f32), square,
            pltpu.VMEM((2, W, L), f32), pltpu.VMEM((2, 2, W, L), f32),
            small, small, small, small, small,
            dma((3, CHUNKS)), dma((3, CHUNKS)), dma((3, CHUNKS)), dma((3, CHUNKS)),
            dma((4,)), dma((4,)), dma((2, 2)), dma((2, 2)),
        ],
        compiler_params=pltpu.CompilerParams(
            collective_id=0, has_side_effects=True, vmem_limit_bytes=62 << 20
        ),
        name="both_applies",
    )(
        rhs.reshape(W, L), coupling.reshape(W, L), fwd_coupling.reshape(W * W, L),
        bwd_coupling.reshape(W * W, L), block_inverse.reshape(W * W, L),
    )
    return corr.reshape(rhs.shape), rem.reshape(rhs.shape)


def solution(mesh):
    vector = P("azim", None, "axial", None)
    matrix = P("azim", None, None, "axial", None)
    return jax.shard_map(
        on_device,
        mesh=mesh,
        in_specs=(vector, vector, matrix, matrix, matrix),
        out_specs=(vector, vector),
        check_vma=False,
    )
```

time: 150 us -> 123 us (0.82)
  Pallas kernels: 143 us -> 121 us
  local copies, waits for them, and re-layouts: 5.88 us -> 1.96 us
    pallas_call x1, Pallas kernels: 143 us -> 121 us  [on_device(): pl.pallas_call(kernel, out_shape=(jax.ShapeDtypeStruct((W, L), f32),) * 2...]
    unnamed x12 -> x4, local copies, waits for them, and re-layouts: 5.88 us -> 1.96 us
where the time goes in v2:
time: 123 us
  Pallas kernels  121 us (98%)
  local copies, waits for them, and re-layouts  1.96 us (2%)
    pallas_call x1, Pallas kernels, on_device(): pl.pallas_call(kernel, out_shape=(jax.ShapeDtypeStruct((W, L), f32),) * 2...  121 us

profile of v2, /device:TPU:1, one launch (start us, length us, event | category | flops | bytes accessed | tf_op | source)
XLA Modules:
  0.0 123.2 jit_solution(453704095514965211)
XLA Ops:
  0.6 120.6 %both_applies.1 = (f32[48,128]{1,0:T(8,128)}, f32[48,128]{1,0:T(8,128)}) custom-call(f32[48,128]{1,0:T(8,128)} %bitcast.14, f32[48,128]{1,0:T(8,128)} %bitcast.15, bf16[2304,128]{1,0:T(8,128)(2,1)} %bitcast.11, bf16[2304,128]{1,0:T(8,128)(2,1)} %bitcast.12, bf16[2304,128]{1,0:T(8,128)(2,1)} %bitcast.13), custom_call_target="tpu_custom_call" | custom-call | tf_op jit(solution)/shard_map/both_applies/pallas_call | solution.py:347
  121.2 0.0 copy-start
  121.2 1.4 %copy.11 = f32[1,48,1,128]{3,2,1,0:T(1,128)} copy(f32[1,48,1,128]{3,2,1,0:T(1,128)} %bitcast.17) | data formatting | bytes 49152
  122.6 0.0 copy-done
  122.6 0.6 copy.12
Async XLA Ops:
  121.2 1.4 %copy-start = (f32[48,128]{1,0:T(8,128)S(1)}, f32[48,128]{1,0:T(8,128)}, u32[]{:S(2)}) copy-start(f32[48,128]{1,0:T(8,128)} %get-tuple-element.5) | copy-start | bytes 73732

commit v3 on v2

v3 whole, which is shorter than its diff:
```python
import functools

import jax
import jax.numpy as jnp
from jax import lax
from jax.experimental import pallas as pl
from jax.experimental.pallas import tpu as pltpu
from jax.sharding import PartitionSpec as P

MESH = pl.DeviceIdType.MESH
W = 48
L = 128
RUN = 8
PIECES = W * W // L
ROWS = PIECES * 16
PARTS = ((0, 9), (9, 6), (15, 3))
CHUNKS = len(PARTS)
FWD, BWD, INV = 0, 1, 2


def aligned(start, size):
    return pl.ds(start if isinstance(start, int) else pl.multiple_of(start, 8), size)


def part_rows(base, chunk):
    first, count = PARTS[chunk]
    return aligned(base + first * 16, count * 16)


def wait_bytes(ref, sem):
    pltpu.make_async_copy(ref, ref, sem).wait()


def matvec(load, vec_ref):
    acc = jnp.zeros((6, 8, L), jnp.float32)
    for a in range(W):
        acc = acc + load(a).reshape(6, 8, L) * vec_ref[pl.ds(a, 8, stride=0), :][None]
    return acc.reshape(W, L)


def kernel(
    rhs_in, coup_in, fwd_in, bwd_in, inv_in, corr, rem, rhs, coup, blocks, in_sem,
    s1, r1, s2, r2, maps, early, dup, packed, inv_t,
    vec, stage, turn, z_out, z_in, g_out, g_in, halo_out, halo_in,
    c_t, rhs_t, coup_t, first, middle,
    mz_send, mz_recv, mg_send, mg_recv, zv_send, zv_recv, gv_send, gv_recv, h_send, h_recv,
):
    me = lax.axis_index("azim")
    station = lax.axis_index("axial")
    z = lax.rem(me, RUN)
    g = me // RUN
    loads = [
        pltpu.make_async_copy(src, dst, in_sem.at[at])
        for at, (src, dst) in enumerate((
            (fwd_in, blocks.at[FWD]), (rhs_in, rhs), (coup_in, coup), (inv_in, blocks.at[INV]), (bwd_in, blocks.at[BWD]),
        ))
    ]
    for load in loads:
        load.start()

    def z_peer(i):
        return {"azim": g * RUN + lax.rem(z + i, RUN)}

    def g_peer(i):
        return {"azim": lax.rem(g + i, RUN) * RUN + z}

    up = {"axial": lax.rem(station + 1, 4)}
    down = {"axial": lax.rem(station + 3, 4)}

    lane = lax.broadcasted_iota(jnp.int32, (W, L), 1)
    lane_z = lax.rem(lane, RUN)
    lane_g = lane // 16

    barrier = pltpu.get_barrier_semaphore()

    def greet(i, _):
        pl.semaphore_signal(barrier, inc=1, device_id=z_peer(i), device_id_type=MESH)
        pl.semaphore_signal(barrier, inc=1, device_id=g_peer(i), device_id_type=MESH)
        return 0

    lax.fori_loop(1, RUN, greet, 0)
    pl.semaphore_signal(barrier, inc=1, device_id=up, device_id_type=MESH)
    pl.semaphore_signal(barrier, inc=1, device_id=down, device_id_type=MESH)

    def remote(src, dst, send, recv, device):
        pltpu.make_async_remote_copy(
            src_ref=src, dst_ref=dst, send_sem=send, recv_sem=recv,
            device_id=device, device_id_type=MESH,
        ).start()

    def pack(kind, chunk):
        def body(step, _):
            for inner in range(3):
                t = step * 3 + inner
                piece = blocks[kind, pl.ds(pl.multiple_of(t * L, L), L), :].astype(jnp.float32).T
                for zo in range(RUN):
                    s1[kind, aligned(zo * ROWS + t * 16, 16)] = piece[zo * 16 : zo * 16 + 16]
            return 0

        lax.fori_loop(PARTS[chunk][0] // 3, sum(PARTS[chunk]) // 3, body, 0)

    def send_z(kind, chunk):
        for i in range(1, RUN):
            to = lax.rem(z + i, RUN)
            remote(
                s1.at[kind, part_rows(to * ROWS, chunk)],
                r1.at[kind, part_rows(z * ROWS, chunk)],
                mz_send.at[kind, chunk], mz_recv.at[kind, chunk], z_peer(i),
            )
        own = part_rows(z * ROWS, chunk)
        r1[kind, own] = s1[kind, own]

    def forward_g(kind, chunk):
        wait_bytes(r1.at[kind, pl.ds(0, 7 * 16 * PARTS[chunk][1])], mz_recv.at[kind, chunk])

        def body(t, _):
            for q in range(16):
                s2[kind, aligned((q // 2) * ROWS + t * 16 + (q % 2) * 8, 8)] = r1[
                    kind, pl.ds(t * 16 + q, 8, stride=ROWS), :
                ]
            return 0

        lax.fori_loop(PARTS[chunk][0], sum(PARTS[chunk]), body, 0)
        send_g(kind, chunk)

    def pack_g(kind, chunk):
        def body(t, _):
            turn[0, 0:L] = blocks[kind, pl.ds(pl.multiple_of(t * L, L), L), :].astype(jnp.float32).T
            for q in range(16):
                s2[kind, aligned((q // 2) * ROWS + t * 16 + (q % 2) * 8, 8)] = turn[0, pl.ds(q, 8, stride=16), :]
            return 0

        lax.fori_loop(PARTS[chunk][0], sum(PARTS[chunk]), body, 0)
        send_g(kind, chunk)

    def send_g(kind, chunk):
        for i in range(1, RUN):
            to = lax.rem(g + i, RUN)
            remote(
                s2.at[kind, part_rows(to * ROWS, chunk)],
                r2.at[kind, part_rows(g * ROWS, chunk)],
                mg_send.at[kind, chunk], mg_recv.at[kind, chunk], g_peer(i),
            )
        own = part_rows(g * ROWS, chunk)
        r2[kind, own] = s2[kind, own]

    def unpack(kind, chunk):
        wait_bytes(r2.at[kind, pl.ds(0, 7 * 16 * PARTS[chunk][1])], mg_recv.at[kind, chunk])

        def body(step, _):
            for inner in range(3):
                t = step * 3 + inner
                rows = [r2[kind, aligned(run * ROWS + t * 16, 16)] for run in range(RUN)]
                piece = jnp.concatenate(rows, axis=0).T
                if kind == INV:
                    inv_t[pl.ds(pl.multiple_of(t * L, L), L), :] = piece
                else:
                    maps[kind, 0, pl.ds(pl.multiple_of(t * L, L), L), :] = -piece
            return 0

        lax.fori_loop(PARTS[chunk][0] // 3, sum(PARTS[chunk]) // 3, body, 0)

    def earlier(value, distance, kind):
        return pltpu.roll(value, distance if kind == FWD else L - distance, 1)

    def inside(distance, kind):
        return lane_z >= distance if kind == FWD else lane_z < RUN - distance

    def compose(kind, level):
        distance = 1 << level
        exists = inside(distance, kind)
        sub = lax.broadcasted_iota(jnp.int32, (W, L), 0)

        def shift(step, _):
            for inner in range(8):
                a = step * 8 + inner
                moved = earlier(maps[kind, level, aligned(a * W, W)], distance, kind)
                early[aligned(a * W, W)] = jnp.where(exists, moved, jnp.where(sub == a, 1.0, 0.0))
            return 0

        lax.fori_loop(0, W // 8, shift, 0)

        def product(four, _):
            acc = [jnp.zeros((6, 8, L), jnp.float32)] * 4
            for c in range(W):
                later = maps[kind, level, pl.ds(c * W, W)].reshape(6, 8, L)
                for i in range(4):
                    factor = early[pl.ds((four * 4 + i) * W + c, 8, stride=0), :]
                    acc[i] = acc[i] + later * factor[None]
            for i in range(4):
                maps[kind, level + 1, aligned((four * 4 + i) * W, W)] = acc[i].reshape(W, L)
            return 0

        lax.fori_loop(0, W // 4, product, 0)

    even = lane_z % 2 == 0
    low2 = lane_z % 4 < 2
    low4 = lane_z < 4
    share = (0, 24, 12, 36)

    def back(value, distance):
        return pltpu.roll(value, L - distance, 1)

    def ahead(value, distance):
        return pltpu.roll(value, distance, 1)

    def rows_of(ref, a):
        return ref[aligned(a * W, W)]

    def each(start, stop, width, do):
        def body(step, _):
            for inner in range(width):
                do(step * width + inner)
            return 0

        lax.fori_loop(start // width, stop // width, body, 0)

    def packed_product(start, stop, width, over, more=False):
        def body(step, _):
            places = [aligned((step * width + i) * W, W) for i in range(width)]
            zero = jnp.zeros((6, 8, L), jnp.float32)
            acc = [packed[place].reshape(6, 8, L) if more else zero for place in places]
            for c in over:
                later = dup[pl.ds(c * W, W)].reshape(6, 8, L)
                for i in range(width):
                    factor = early[pl.ds((step * width + i) * W + c, 8, stride=0), :]
                    acc[i] = acc[i] + later * factor[None]
            for i in range(width):
                packed[places[i]] = acc[i].reshape(W, L)
            return 0

        lax.fori_loop(start // width, stop // width, body, 0)

    one, two, four, eight = (maps.at[BWD, level] for level in range(4))

    def early_pair(a):
        early[aligned(a * W, W)] = jnp.where(even, back(rows_of(one, a), 1), rows_of(one, a + 24))

    def later_pair(c):
        value = rows_of(one, c)
        dup[aligned(c * W, W)] = jnp.where(even, value, ahead(value, 1))

    def tree_start():
        each(0, 16, 8, early_pair)
        each(0, 40, 8, later_pair)
        packed_product(0, 16, 4, range(40))

    def tree_rest():
        each(16, 24, 8, early_pair)
        each(40, 48, 8, later_pair)
        packed_product(0, 16, 4, range(40, 48), True)
        packed_product(16, 24, 4, range(48))

        def early_quad(a):
            early[aligned(a * W, W)] = jnp.where(low2, back(rows_of(packed, a), 2), rows_of(packed, a + 12))

        def full_pair(a):
            value = rows_of(packed, a)
            for at, full in ((a, jnp.where(even, value, ahead(value, 1))), (a + 24, jnp.where(even, back(value, 1), value))):
                two[aligned(at * W, W)] = full
                dup[aligned(at * W, W)] = jnp.where(low2, full, ahead(full, 2))

        each(0, 12, 6, early_quad)
        each(0, 24, 4, full_pair)
        packed_product(0, 12, 4, range(48))

        def early_eight(a):
            early[aligned(a * W, W)] = jnp.where(low4, back(rows_of(packed, a), 4), rows_of(packed, a + 6))

        def full_quad(a):
            value = rows_of(packed, a)
            evens = jnp.where(even, value, ahead(value, 1))
            odds = jnp.where(even, back(value, 1), value)
            for q, pair in enumerate((evens, odds, evens, odds)):
                full = jnp.where(low2, pair, ahead(pair, 2)) if q < 2 else jnp.where(low2, back(pair, 2), pair)
                four[aligned((a + share[q]) * W, W)] = full
                dup[aligned((a + share[q]) * W, W)] = jnp.where(low4, full, ahead(full, 4))

        each(0, 6, 6, early_eight)
        each(0, 12, 2, full_quad)
        packed_product(0, 6, 3, range(48))

        def full_eight(a):
            value = rows_of(packed, a)
            for zz in range(RUN):
                full = back(value, zz) if zz else value
                at = a + share[zz % 4] + (6 if zz >= 4 else 0)
                eight[aligned(at * W, W)] = jnp.where(lane_z == 4, rows_of(four, at), full)

        each(0, 6, 2, full_eight)

    def tree_sweep(value):
        def add(state, level, entering):
            vec[0:W] = entering
            return state + apply_map(BWD, level)

        state = add(value, 0, jnp.where(even, back(value, 1), 0.0))
        state = add(state, 1, jnp.where(lane_z % 4 == 0, back(state, 2), 0.0))
        state = add(state, 2, jnp.where(lane_z == 0, back(state, 4), 0.0))

        def run_step(n, carry):
            running, entering = carry
            moved = jnp.where(lane_z == 0, back(running, 16), 0.0)
            entering = jnp.where(RUN - 1 - lane_g == n - RUN, moved, entering)
            return add(state, 3, moved), entering

        running, entering = lax.fori_loop(1, 15, run_step, (state, jnp.zeros((W, L), jnp.float32)))
        entering = jnp.where(lane_g == 0, back(running, 16), entering)
        entering = jnp.where(lane_z == 0, entering, 0.0)
        at_four, at_six, at_seven = (ahead(entering, d) for d in (4, 6, 7))
        state = add(state, 3, entering + at_four)
        state = add(state, 1, jnp.where(lane_z == 2, back(state, 2), at_six))
        return add(state, 0, jnp.where(even, 0.0, jnp.where(lane_z == 7, at_seven, back(state, 1))))

    def apply_map(kind, level):
        return matvec(lambda a: maps[kind, level, pl.ds(a * W, W)], vec)

    def sweep(kind, value):
        state = value
        for level in range(3):
            distance = 1 << level
            moved = earlier(state, distance, kind)
            vec[0:W] = jnp.where(inside(distance, kind), moved, 0.0)
            state = state + apply_map(kind, level)
        order = lane_g if kind == FWD else RUN - 1 - lane_g

        def run_step(n, carry):
            running, entering = carry
            moved = earlier(running, 16, kind)
            entering = jnp.where(order == n - RUN, moved, entering)
            vec[0:W] = moved
            return state + apply_map(kind, 3), entering

        running, entering = lax.fori_loop(1, 15, run_step, (state, jnp.zeros((W, L), jnp.float32)))
        entering = jnp.where(order == RUN - 1, earlier(running, 16, kind), entering)
        place = RUN - 1 - lane_z if kind == FWD else lane_z
        for distance in (1, 2, 4):
            back = pltpu.roll(entering, L - distance if kind == FWD else distance, 1)
            entering = jnp.where(place < distance, entering, back)
        vec[0:W] = entering
        return state + apply_map(kind, 3)

    def g_stage(at, gather):
        for run in range(RUN):
            for half in range(2):
                g_out[at, run * 16 + half * 8 : run * 16 + half * 8 + 8] = gather(run, half)
        for i in range(1, RUN):
            to = lax.rem(g + i, RUN)
            remote(
                g_out.at[at, aligned(to * 16, 16)], g_in.at[at, aligned(g * 16, 16)],
                gv_send.at[at], gv_recv.at[at], g_peer(i),
            )
        g_in[at, aligned(g * 16, 16)] = g_out[at, aligned(g * 16, 16)]

    def z_start(at, value):
        stage[0:W] = value
        turn[0, 0:L] = stage[...].T
        for zz in range(RUN):
            for half in range(2):
                z_out[at, pl.ds(zz * 16 + half * 8, 8)] = turn[0, pl.ds(zz + 64 * half, 8, stride=8), :]
        for i in (4, 3, 5, 2, 6, 1, 7):
            to = lax.rem(z + i, RUN)
            remote(
                z_out.at[at, aligned(to * 16, 16)], z_in.at[at, aligned(z * 16, 16)],
                zv_send.at[at], zv_recv.at[at], z_peer(i),
            )
        z_in[at, aligned(z * 16, 16)] = z_out[at, aligned(z * 16, 16)]

    def z_finish(at):
        wait_bytes(z_in.at[at, pl.ds(0, 7 * 16)], zv_recv.at[at])
        for m in range(16):
            turn[0, m * 8 : m * 8 + 8] = z_in[at, pl.ds(m, 8, stride=16), :]
        return turn[0, 0:L].T[0:W]

    def stations_start(at, value):
        halo_out[at] = value
        remote(halo_out.at[at], halo_in.at[at, 0], h_send.at[at, 0], h_recv.at[at, 0], up)
        remote(halo_out.at[at], halo_in.at[at, 1], h_send.at[at, 1], h_recv.at[at, 1], down)

    def stations_finish(at):
        for side in range(2):
            wait_bytes(halo_in.at[at, side], h_recv.at[at, side])
            wait_bytes(halo_out.at[at], h_send.at[at, side])
        below = jnp.where(station > 0, halo_in[at, 0], 0.0)
        above = jnp.where(station < 3, halo_in[at, 1], 0.0)
        return below + above

    def inverse(ref):
        return matvec(lambda a: inv_t[pl.ds(a * W, W)], ref)

    loads[0].wait()
    for chunk in range(CHUNKS):
        pack(FWD, chunk)
        if chunk == 0:
            pl.semaphore_wait(barrier, 16)
        send_z(FWD, chunk)
    for load in loads[1:]:
        load.wait()
    vec[0:W] = rhs[...]
    stage[...] = jnp.zeros((L, L), jnp.float32)
    stage[0:W] = matvec(lambda a: blocks[INV, pl.ds(a * W, W), :].astype(jnp.float32), vec)
    stage[W : 2 * W] = rhs[...]
    turn[0, 0:L] = stage[...].T
    g_stage(0, lambda run, half: turn[0, pl.ds(run * 2 + half, 8, stride=16), :])
    stage[0:W] = coup[...]
    turn[1, 0:L] = stage[...].T
    g_stage(2, lambda run, half: turn[1, pl.ds(run * 2 + half, 8, stride=16), :])
    for chunk in range(CHUNKS):
        pack(BWD, chunk)
    wait_bytes(g_in.at[0, pl.ds(0, 7 * 16)], gv_recv.at[0])
    turned = g_in[0].T
    rhs_t[...] = turned[W : 2 * W]
    z_start(0, turned[0:W])
    for chunk in range(CHUNKS):
        pack_g(INV, chunk)
    for chunk in range(CHUNKS):
        send_z(BWD, chunk)
    for chunk in range(CHUNKS):
        forward_g(FWD, chunk)
    for chunk in range(CHUNKS):
        unpack(FWD, chunk)
    compose(FWD, 0)
    compose(FWD, 1)
    forward_g(BWD, 0)
    wait_bytes(g_in.at[2, pl.ds(0, 7 * 16)], gv_recv.at[2])
    coup_t[...] = g_in[2].T[0:W]
    for chunk in range(CHUNKS):
        unpack(INV, chunk)
    compose(FWD, 2)
    c_t[...] = z_finish(0)
    c_t[...] = sweep(FWD, c_t[...])
    forward_g(BWD, 1)
    forward_g(BWD, 2)
    unpack(BWD, 0)
    unpack(BWD, 1)
    tree_start()
    unpack(BWD, 2)
    tree_rest()

    z_start(1, tree_sweep(c_t[...]))
    first[...] = z_finish(1)
    stations_start(0, first[...])
    vec[0:W] = rhs_t[...] - first[...] + coup_t[...] * stations_finish(0)
    middle[...] = vec[0:W]
    z_start(2, inverse(vec))
    c_t[...] = z_finish(2)
    c_t[...] = sweep(FWD, c_t[...])
    z_start(3, tree_sweep(c_t[...]))
    c_t[...] = z_finish(3)
    stations_start(1, c_t[...])
    stage[0:W] = first[...] + c_t[...]
    stage[W : 2 * W] = middle[...] - c_t[...] + coup_t[...] * stations_finish(1)
    turn[0, 0:L] = stage[...].T
    g_stage(1, lambda run, half: turn[0, pl.ds(run * 16 + half * 8, 8)])
    wait_bytes(g_in.at[1, pl.ds(0, 7 * 16)], gv_recv.at[1])
    for q in range(16):
        turn[1, pl.ds(q, 8, stride=16), :] = g_in[1, pl.ds(q * 8, 8)]
    final = turn[1, 0:L].T
    corr[...] = final[0:W]
    rem[...] = final[W : 2 * W]

    for kind in range(3):
        for chunk in range(CHUNKS):
            if kind != INV:
                wait_bytes(s1.at[kind, pl.ds(0, 7 * 16 * PARTS[chunk][1])], mz_send.at[kind, chunk])
            wait_bytes(s2.at[kind, pl.ds(0, 7 * 16 * PARTS[chunk][1])], mg_send.at[kind, chunk])
    for at in range(4):
        wait_bytes(z_out.at[at, pl.ds(0, 7 * 16)], zv_send.at[at])
    for at in range(3):
        wait_bytes(g_out.at[at, pl.ds(0, 7 * 16)], gv_send.at[at])


def on_device(rhs, coupling, fwd_coupling, bwd_coupling, block_inverse):
    f32 = jnp.float32
    vmem = pl.BlockSpec(memory_space=pltpu.VMEM)
    dma = pltpu.SemaphoreType.DMA
    mat = pltpu.VMEM((3, W * W, L), f32)
    small = pltpu.VMEM((W, L), f32)
    corr, rem = pl.pallas_call(
        kernel,
        out_shape=(jax.ShapeDtypeStruct((W, L), f32),) * 2,
        in_specs=[pl.BlockSpec(memory_space=pl.ANY)] * 5,
        out_specs=(vmem, vmem),
        scratch_shapes=[
            small, small, pltpu.VMEM((3, W * W, L), jnp.bfloat16), dma((5,)),
            pltpu.VMEM((2, W * W, L), f32), pltpu.VMEM((2, W * W + ROWS, L), f32), mat, mat,
            pltpu.VMEM((2, 4, W * W, L), f32), pltpu.VMEM((W * W + 8, L), f32), pltpu.VMEM((W * W, L), f32),
            pltpu.VMEM((W * W // 2, L), f32), pltpu.VMEM((W * W, L), f32),
            pltpu.VMEM((W + 8, L), f32), pltpu.VMEM((L, L), f32), pltpu.VMEM((2, L + 16, L), f32),
            pltpu.VMEM((4, L, L), f32), pltpu.VMEM((4, L + 16, L), f32),
            pltpu.VMEM((3, L, L), f32), pltpu.VMEM((3, L, L), f32),
            pltpu.VMEM((2, W, L), f32), pltpu.VMEM((2, 2, W, L), f32),
            small, small, small, small, small,
            dma((2, CHUNKS)), dma((2, CHUNKS)), dma((3, CHUNKS)), dma((3, CHUNKS)),
            dma((4,)), dma((4,)), dma((3,)), dma((3,)), dma((2, 2)), dma((2, 2)),
        ],
        compiler_params=pltpu.CompilerParams(
            collective_id=0, has_side_effects=True, vmem_limit_bytes=62 << 20
        ),
        name="both_applies",
    )(
        rhs.reshape(W, L), coupling.reshape(W, L), fwd_coupling.reshape(W * W, L),
        bwd_coupling.reshape(W * W, L), block_inverse.reshape(W * W, L),
    )
    return corr.reshape(rhs.shape), rem.reshape(rhs.shape)


def solution(mesh):
    vector = P("azim", None, "axial", None)
    matrix = P("azim", None, None, "axial", None)
    return jax.shard_map(
        on_device,
        mesh=mesh,
        in_specs=(vector, vector, matrix, matrix, matrix),
        out_specs=(vector, vector),
        check_vma=False,
    )
```

time: 123 us -> 116 us (0.943)
  Pallas kernels: 121 us -> 113 us
    pallas_call x1, Pallas kernels: 121 us -> 113 us  [on_device(): pl.pallas_call(kernel, out_shape=(jax.ShapeDtypeStruct((W, L), f32),) * 2...]
where the time goes in v3:
time: 116 us
  Pallas kernels  113 us (97%)
  local copies, waits for them, and re-layouts  1.96 us (2%)
    pallas_call x1, Pallas kernels, on_device(): pl.pallas_call(kernel, out_shape=(jax.ShapeDtypeStruct((W, L), f32),) * 2...  113 us

profile of v3, /device:TPU:1, one launch (start us, length us, event | category | flops | bytes accessed | tf_op | source)
XLA Modules:
  0.0 115.6 jit_solution(13927521058695574284)
XLA Ops:
  0.6 113.0 %both_applies.1 = (f32[48,128]{1,0:T(8,128)}, f32[48,128]{1,0:T(8,128)}) custom-call(f32[48,128]{1,0:T(8,128)} %bitcast.14, f32[48,128]{1,0:T(8,128)} %bitcast.15, bf16[2304,128]{1,0:T(8,128)(2,1)} %bitcast.11, bf16[2304,128]{1,0:T(8,128)(2,1)} %bitcast.12, bf16[2304,128]{1,0:T(8,128)(2,1)} %bitcast.13), custom_call_target="tpu_custom_call" | custom-call | tf_op jit(solution)/shard_map/both_applies/pallas_call | solution.py:479
  113.7 0.0 copy-start
  113.7 1.4 %copy.11 = f32[1,48,1,128]{3,2,1,0:T(1,128)} copy(f32[1,48,1,128]{3,2,1,0:T(1,128)} %bitcast.17) | data formatting | bytes 49152
  115.0 0.0 copy-done
  115.0 0.6 copy.12
Async XLA Ops:
  113.7 1.4 %copy-start = (f32[48,128]{1,0:T(8,128)S(1)}, f32[48,128]{1,0:T(8,128)}, u32[]{:S(2)}) copy-start(f32[48,128]{1,0:T(8,128)} %get-tuple-element.5) | copy-start | bytes 73732

commit v4 on v3

--- a/solution.py
+++ b/solution.py
@@ -39,7 +39,7 @@
 
 
 def kernel(
-    rhs_in, coup_in, fwd_in, bwd_in, inv_in, corr, rem, rhs, coup, blocks, in_sem,
+    rhs_in, coup_in, fwd_in, bwd_in, inv_in, lines, rhs, coup, blocks, in_sem,
     s1, r1, s2, r2, maps, early, dup, packed, inv_t,
     vec, stage, turn, z_out, z_in, g_out, g_in, halo_out, halo_in,
     c_t, rhs_t, coup_t, first, middle,
@@ -164,10 +164,12 @@
         return pltpu.roll(value, distance if kind == FWD else L - distance, 1)
 
     def inside(distance, kind):
+        if distance >= 16:
+            return lane_g >= distance // 16
         return lane_z >= distance if kind == FWD else lane_z < RUN - distance
 
     def compose(kind, level):
-        distance = 1 << level
+        distance = 1 << level if level < 3 else 16 << (level - 3)
         exists = inside(distance, kind)
         sub = lax.broadcasted_iota(jnp.int32, (W, L), 0)
 
@@ -192,6 +194,31 @@
             return 0
 
         lax.fori_loop(0, W // 4, product, 0)
+
+    def paired_sweep(value):
+        def add(state, level, entering):
+            vec[0:W] = entering
+            return state + apply_map(FWD, level)
+
+        def moved(state, distance):
+            return jnp.where(inside(distance, FWD), pltpu.roll(state, distance, 1), 0.0)
+
+        state = value
+        for level in range(3):
+            state = add(state, level, moved(state, 1 << level))
+        two_runs = add(state, 3, moved(state, 16))
+        four_runs = add(two_runs, 4, moved(two_runs, 32))
+        turn_end = pltpu.roll(add(four_runs, 5, moved(four_runs, 64)), 16, 1)
+        wrapped = turn_end
+        for runs in (1, 2, 4):
+            wrapped = jnp.where(lane_g < runs, wrapped, pltpu.roll(wrapped, 16 * runs, 1))
+        low = add(four_runs, 5, wrapped)
+        high = add(four_runs, 5, pltpu.roll(low, 64, 1))
+        leaving = jnp.where(lane_g < 4, low, high)
+        entering = jnp.where(lane_g == 0, turn_end, pltpu.roll(leaving, 16, 1))
+        for distance in (1, 2, 4):
+            entering = jnp.where(RUN - 1 - lane_z < distance, entering, pltpu.roll(entering, L - distance, 1))
+        return add(state, 3, entering)
 
     even = lane_z % 2 == 0
     low2 = lane_z % 4 < 2
@@ -438,13 +465,15 @@
     tree_rest()
 
     z_start(1, tree_sweep(c_t[...]))
+    compose(FWD, 3)
     first[...] = z_finish(1)
     stations_start(0, first[...])
     vec[0:W] = rhs_t[...] - first[...] + coup_t[...] * stations_finish(0)
     middle[...] = vec[0:W]
     z_start(2, inverse(vec))
+    compose(FWD, 4)
     c_t[...] = z_finish(2)
-    c_t[...] = sweep(FWD, c_t[...])
+    c_t[...] = paired_sweep(c_t[...])
     z_start(3, tree_sweep(c_t[...]))
     c_t[...] = z_finish(3)
     stations_start(1, c_t[...])
@@ -455,9 +484,7 @@
     wait_bytes(g_in.at[1, pl.ds(0, 7 * 16)], gv_recv.at[1])
     for q in range(16):
         turn[1, pl.ds(q, 8, stride=16), :] = g_in[1, pl.ds(q * 8, 8)]
-    final = turn[1, 0:L].T
-    corr[...] = final[0:W]
-    rem[...] = final[W : 2 * W]
+    lines[...] = turn[1, 0:L]
 
     for kind in range(3):
         for chunk in range(CHUNKS):
@@ -470,21 +497,27 @@
         wait_bytes(g_out.at[at, pl.ds(0, 7 * 16)], gv_send.at[at])
 
 
+def outputs(lines, corr, rem):
+    final = lines[...].T
+    corr[...] = final[0:W]
+    rem[...] = final[W : 2 * W]
+
+
 def on_device(rhs, coupling, fwd_coupling, bwd_coupling, block_inverse):
     f32 = jnp.float32
     vmem = pl.BlockSpec(memory_space=pltpu.VMEM)
     dma = pltpu.SemaphoreType.DMA
     mat = pltpu.VMEM((3, W * W, L), f32)
     small = pltpu.VMEM((W, L), f32)
-    corr, rem = pl.pallas_call(
+    lines = pl.pallas_call(
         kernel,
-        out_shape=(jax.ShapeDtypeStruct((W, L), f32),) * 2,
+        out_shape=jax.ShapeDtypeStruct((L, L), f32),
         in_specs=[pl.BlockSpec(memory_space=pl.ANY)] * 5,
-        out_specs=(vmem, vmem),
+        out_specs=vmem,
         scratch_shapes=[
             small, small, pltpu.VMEM((3, W * W, L), jnp.bfloat16), dma((5,)),
             pltpu.VMEM((2, W * W, L), f32), pltpu.VMEM((2, W * W + ROWS, L), f32), mat, mat,
-            pltpu.VMEM((2, 4, W * W, L), f32), pltpu.VMEM((W * W + 8, L), f32), pltpu.VMEM((W * W, L), f32),
+            pltpu.VMEM((2, 6, W * W, L), f32), pltpu.VMEM((W * W + 8, L), f32), pltpu.VMEM((W * W, L), f32),
             pltpu.VMEM((W * W // 2, L), f32), pltpu.VMEM((W * W, L), f32),
             pltpu.VMEM((W + 8, L), f32), pltpu.VMEM((L, L), f32), pltpu.VMEM((2, L + 16, L), f32),
             pltpu.VMEM((4, L, L), f32), pltpu.VMEM((4, L + 16, L), f32),
@@ -502,6 +535,13 @@
         rhs.reshape(W, L), coupling.reshape(W, L), fwd_coupling.reshape(W * W, L),
         bwd_coupling.reshape(W * W, L), block_inverse.reshape(W * W, L),
     )
+    corr, rem = pl.pallas_call(
+        outputs,
+        out_shape=(jax.ShapeDtypeStruct((W, L), f32),) * 2,
+        in_specs=[vmem],
+        out_specs=(vmem, vmem),
+        name="outputs",
+    )(lines)
     return corr.reshape(rhs.shape), rem.reshape(rhs.shape)
 
 

time: 116 us -> 114 us (0.983)
  local copies, waits for them, and re-layouts: 1.96 us -> 0 us
    unnamed x4 -> x0, local copies, waits for them, and re-layouts: 1.96 us -> none
    pallas_call x1 -> x2, Pallas kernels: 113 us -> 114 us  [the longest x1 112 us: on_device(): pl.pallas_call(kernel, out_shape=jax.ShapeDtypeStruct((L, L), f32), in_sp...]
where the time goes in v4:
time: 114 us
  Pallas kernels  114 us (100%)
    pallas_call x1, Pallas kernels, on_device(): pl.pallas_call(kernel, out_shape=jax.ShapeDtypeStruct((L, L), f32), in_sp...  112 us

profile of v4, /device:TPU:1, one launch (start us, length us, event | category | flops | bytes accessed | tf_op | source)
XLA Modules:
  0.0 114.3 jit_solution(17911966004217737841)
XLA Ops:
  0.6 112.1 %both_applies.1.lines = f32[128,128]{1,0:T(8,128)} custom-call(f32[48,128]{1,0:T(8,128)} %bitcast.14, f32[48,128]{1,0:T(8,128)} %bitcast.15, bf16[2304,128]{1,0:T(8,128)(2,1)} %bitcast.11, bf16[2304,128]{1,0:T(8,128)(2,1)} %bitcast.12, bf16[2304,128]{1,0:T(8,128)(2,1)} %bitcast.13), custom_call_target="tpu_custom_call" | custom-call | tf_op jit(solution)/shard_map/both_applies/pallas_call | solution.py:512
  112.7 1.5 %outputs.1 = (f32[48,128]{1,0:T(8,128)}, f32[48,128]{1,0:T(8,128)}) custom-call(f32[128,128]{1,0:T(8,128)} %both_applies.1.lines), custom_call_target="tpu_custom_call" | custom-call | tf_op jit(solution)/shard_map/outputs/pallas_call | solution.py:538

commit v5 on v4

--- a/solution.py
+++ b/solution.py
@@ -439,9 +439,9 @@
     rhs_t[...] = turned[W : 2 * W]
     z_start(0, turned[0:W])
     for chunk in range(CHUNKS):
+        send_z(BWD, chunk)
+    for chunk in range(CHUNKS):
         pack_g(INV, chunk)
-    for chunk in range(CHUNKS):
-        send_z(BWD, chunk)
     for chunk in range(CHUNKS):
         forward_g(FWD, chunk)
     for chunk in range(CHUNKS):
@@ -449,10 +449,6 @@
     compose(FWD, 0)
     compose(FWD, 1)
     forward_g(BWD, 0)
-    wait_bytes(g_in.at[2, pl.ds(0, 7 * 16)], gv_recv.at[2])
-    coup_t[...] = g_in[2].T[0:W]
-    for chunk in range(CHUNKS):
-        unpack(INV, chunk)
     compose(FWD, 2)
     c_t[...] = z_finish(0)
     c_t[...] = sweep(FWD, c_t[...])
@@ -468,6 +464,10 @@
     compose(FWD, 3)
     first[...] = z_finish(1)
     stations_start(0, first[...])
+    wait_bytes(g_in.at[2, pl.ds(0, 7 * 16)], gv_recv.at[2])
+    coup_t[...] = g_in[2].T[0:W]
+    for chunk in range(CHUNKS):
+        unpack(INV, chunk)
     vec[0:W] = rhs_t[...] - first[...] + coup_t[...] * stations_finish(0)
     middle[...] = vec[0:W]
     z_start(2, inverse(vec))

time: 114 us -> 114 us (level)
  no operation moved by 1% of the time
where the time goes in v5:
time: 114 us
  Pallas kernels  113 us (99%)
    pallas_call x1, Pallas kernels, on_device(): pl.pallas_call(kernel, out_shape=jax.ShapeDtypeStruct((L, L), f32), in_sp...  112 us

profile of v5, /device:TPU:1, one launch (start us, length us, event | category | flops | bytes accessed | tf_op | source)
XLA Modules:
  0.0 114.0 jit_solution(10871948735380877245)
XLA Ops:
  0.6 111.8 %both_applies.1.lines = f32[128,128]{1,0:T(8,128)} custom-call(f32[48,128]{1,0:T(8,128)} %bitcast.14, f32[48,128]{1,0:T(8,128)} %bitcast.15, bf16[2304,128]{1,0:T(8,128)(2,1)} %bitcast.11, bf16[2304,128]{1,0:T(8,128)(2,1)} %bitcast.12, bf16[2304,128]{1,0:T(8,128)(2,1)} %bitcast.13), custom_call_target="tpu_custom_call" | custom-call | tf_op jit(solution)/shard_map/both_applies/pallas_call | solution.py:512
  112.4 1.5 %outputs.1 = (f32[48,128]{1,0:T(8,128)}, f32[48,128]{1,0:T(8,128)}) custom-call(f32[128,128]{1,0:T(8,128)} %both_applies.1.lines), custom_call_target="tpu_custom_call" | custom-call | tf_op jit(solution)/shard_map/outputs/pallas_call | solution.py:538

commit v6 on v5

--- a/solution.py
+++ b/solution.py
@@ -371,7 +371,7 @@
         for run in range(RUN):
             for half in range(2):
                 g_out[at, run * 16 + half * 8 : run * 16 + half * 8 + 8] = gather(run, half)
-        for i in range(1, RUN):
+        for i in (5, 3, 7, 1, 4, 2, 6):
             to = lax.rem(g + i, RUN)
             remote(
                 g_out.at[at, aligned(to * 16, 16)], g_in.at[at, aligned(g * 16, 16)],
@@ -407,7 +407,6 @@
     def stations_finish(at):
         for side in range(2):
             wait_bytes(halo_in.at[at, side], h_recv.at[at, side])
-            wait_bytes(halo_out.at[at], h_send.at[at, side])
         below = jnp.where(station > 0, halo_in[at, 0], 0.0)
         above = jnp.where(station < 3, halo_in[at, 1], 0.0)
         return below + above
@@ -491,6 +490,9 @@
             if kind != INV:
                 wait_bytes(s1.at[kind, pl.ds(0, 7 * 16 * PARTS[chunk][1])], mz_send.at[kind, chunk])
             wait_bytes(s2.at[kind, pl.ds(0, 7 * 16 * PARTS[chunk][1])], mg_send.at[kind, chunk])
+    for at in range(2):
+        for side in range(2):
+            wait_bytes(halo_out.at[at], h_send.at[at, side])
     for at in range(4):
         wait_bytes(z_out.at[at, pl.ds(0, 7 * 16)], zv_send.at[at])
     for at in range(3):

time: 114 us -> 113 us (level)
  no operation moved by 1% of the time
where the time goes in v6:
time: 113 us
  Pallas kernels  113 us (100%)
    pallas_call x1, Pallas kernels, on_device(): pl.pallas_call(kernel, out_shape=jax.ShapeDtypeStruct((L, L), f32), in_sp...  111 us

profile of v6, /device:TPU:1, one launch (start us, length us, event | category | flops | bytes accessed | tf_op | source)
XLA Modules:
  0.0 113.2 jit_solution(7389089183895879265)
XLA Ops:
  0.6 111.0 %both_applies.1.lines = f32[128,128]{1,0:T(8,128)} custom-call(f32[48,128]{1,0:T(8,128)} %bitcast.14, f32[48,128]{1,0:T(8,128)} %bitcast.15, bf16[2304,128]{1,0:T(8,128)(2,1)} %bitcast.11, bf16[2304,128]{1,0:T(8,128)(2,1)} %bitcast.12, bf16[2304,128]{1,0:T(8,128)(2,1)} %bitcast.13), custom_call_target="tpu_custom_call" | custom-call | tf_op jit(solution)/shard_map/both_applies/pallas_call | solution.py:514
  111.7 1.5 %outputs.1 = (f32[48,128]{1,0:T(8,128)}, f32[48,128]{1,0:T(8,128)}) custom-call(f32[128,128]{1,0:T(8,128)} %both_applies.1.lines), custom_call_target="tpu_custom_call" | custom-call | tf_op jit(solution)/shard_map/outputs/pallas_call | solution.py:540
